TPU v7x, 32 devices: a whole 2x2x4 slice. The times are simulated.
32 devices in a mesh: group: 2 (over y), tile: 4 (over x, core), seq: 4 (over z).
Axes of the slice: x: 2, y: 2, z: 4, core: 2. Of those that a mesh axis runs over, the one named last changes fastest.
Arguments:
- hidden: bfloat16 [8, 1024, 3072], P(('group', 'tile'), 'seq'), parts along dimension 0
- modulation: float32 [10, 3072], P('group'), parts along dimension 0, may hold values from -3 to 3
- w_qkv: bfloat16 [3072, 9216], P('tile', 'seq')
- w_out: bfloat16 [3072, 3072], P('seq', 'tile'), may hold values from -0.109375 to 0.109375
- w_head: bfloat16 [3072, 64], replicated, may hold values from -0.109375 to 0.109375
- latent: float32 [8, 1024, 64], P(('group', 'tile'), 'seq'), parts along dimension 0, may hold values from -6 to 6
- weights_int: int32 [8, 1024], P(('group', 'tile'), 'seq'), parts along dimension 0, may hold values from 1 to 8
- step_index: int32 [2], P('group'), parts along dimension 0, may hold values from 0 to 13
Outputs:
- stepped: float32 [8, 1024, 64], P(('group', 'tile'), 'seq'), parts along dimension 0
- clean: float32 [8, 1024, 64], P(('group', 'tile'), 'seq'), parts along dimension 0
There are 2 independent parts, one for each index of `group`. A program takes and returns all parts, laid end to end along the dimension named above; an argument that names none is the same for every part. Nothing has to cross between parts.
All inputs are finite; a program needn't handle non-finite values.
Results may differ from a plain program's by a relative error of at most 0.0055.
Values may be sent and summed in bfloat16 or wider, within the bound.
A program may use at most 64 MiB of HBM per device.

v0:
```python
import functools
import math

import jax
import jax.numpy as jnp
from jax import lax
from jax.experimental import pallas as pl
from jax.experimental.pallas import tpu as pltpu
from jax.sharding import PartitionSpec as P

HD = 128
NSTEPS = 28


def layer_norm(values):
    mean = jnp.mean(values, axis=-1, keepdims=True)
    centred = values - mean
    spread = jnp.mean(centred * centred, axis=-1, keepdims=True)
    return centred * lax.rsqrt(spread + 1e-06)


def root_norm(values):
    return values * lax.rsqrt(jnp.mean(values * values, axis=-1, keepdims=True) + 1e-06)


def noise_level(index, steps):
    level = 1.0 - index / steps
    return 3.0 * level / (1.0 + 2.0 * level)


MESH = pl.DeviceIdType.MESH


def run(cond, body):
    if cond is None:
        body()
    else:
        pl.when(cond)(body)


def arrives(place, count, way, far):
    return place >= far if way == 0 else place <= count - 1 - far


def goes_on(place, count, way):
    return place < count - 1 if way == 0 else place > 0


def gather_kernel(
    groups, chips, seqs, scale, norm, wq, wo, q_all, o_all, attended,
    n_all, v_wq, v_wo, w_head, queries, keys, values, local, w_sem,
    nz_s, nz_r, oz_s, oz_r, qx_s, qx_r, ox_s, ox_r, qy_s, qy_r, oy_s, oy_r, qc_s, qc_r, oc_s, oc_r,
):
    group, tile, place = lax.axis_index("group"), lax.axis_index("tile"), lax.axis_index("seq")
    chip, core = tile // 2, tile % 2
    other = 1 - core
    partner = {"tile": chip * 2 + other}
    q_rows, o_rows = wq.shape[0] // groups, wo.shape[0] // groups
    both = jnp.logical_and

    def q_part(owner, part):
        return q_all.at[owner, pl.ds(pl.multiple_of(part * q_rows, 8), q_rows)]

    def o_part(owner, row, part):
        return o_all.at[owner, row, pl.ds(pl.multiple_of(part * o_rows, 8), o_rows)]

    def along_seq(way):
        return {"seq": place + 1 - 2 * way}

    def along_chip(way):
        return {"tile": tile + 2 - 4 * way}

    def peer(step):
        return {"group": (group + step) % groups}

    barrier = pltpu.get_barrier_semaphore()
    greet = [(goes_on(place, seqs, way), along_seq(way)) for way in (0, 1)]
    greet += [(goes_on(chip, chips, way), along_chip(way)) for way in (0, 1)]
    greet += [(None, peer(step)) for step in range(1, groups)] + [(None, partner)]
    for cond, device in greet:
        run(cond, lambda device=device: pl.semaphore_signal(barrier, inc=1, device_id=device, device_id_type=MESH))
    met = groups + sum(goes_on(at, count, way).astype(jnp.int32) for at, count in ((place, seqs), (chip, chips)) for way in (0, 1))
    pl.semaphore_wait(barrier, met)

    sent = []

    def copy(source, target, send, recv, device):
        return pltpu.make_async_remote_copy(
            src_ref=source, dst_ref=target, send_sem=send, recv_sem=recv, device_id=device, device_id_type=MESH
        )

    def start(cond, *made):
        run(cond, lambda: copy(*made).start())
        sent.append((cond, made))

    def arrived(cond, target, send, recv, device):
        run(cond, lambda: copy(target, target, send, recv, device).wait_recv())

    def q_to_peers(cond, at, source):
        for step in range(1, groups):
            start(cond, source, q_part(at * 2 + core, group), qy_s.at[at, step], qy_r.at[at, step], peer(step))

    def q_to_partner(cond, at, part, source):
        start(cond, source, q_part(at * 2 + core, part), qc_s.at[at, part], qc_r.at[at, part], partner)

    def o_to_peers(cond, at, row, source):
        for step in range(1, groups):
            start(cond, source, o_part(at * 2 + core, row, group), oy_s.at[at, row, step], oy_r.at[at, row, step], peer(step))

    def o_to_partner(cond, at, row, part, source):
        start(cond, source, o_part(at * 2 + core, row, part), oc_s.at[at, row, part], oc_r.at[at, row, part], partner)

    def o_along_chip(cond, way, far, at, row, source):
        start(cond, source, o_part(at * 2 + core, row, group), ox_s.at[way, far, row], ox_r.at[way, far, row], along_chip(way))

    loads = [pltpu.make_async_copy(a, b, local.at[k]) for k, (a, b) in enumerate(((norm, n_all.at[place]), (wq, v_wq), (wo, v_wo)))]
    for load in loads:
        load.start()

    own_q = wq.at[pl.ds(pl.multiple_of(group * q_rows, 8), q_rows)]
    own_o = wo.at[pl.ds(pl.multiple_of(group * o_rows, 8), o_rows)]
    for way in (0, 1):
        go = goes_on(place, seqs, way)
        start(go, norm, n_all.at[place], nz_s.at[way, 1], nz_r.at[way, 1], along_seq(way))
        start(go, own_o, o_part(tile, place, group), oz_s.at[way, 1], oz_r.at[way, 1], along_seq(way))
        go = goes_on(chip, chips, way)
        start(go, own_q, q_part(tile, group), qx_s.at[way, 1], qx_r.at[way, 1], along_chip(way))
        o_along_chip(go, way, 1, chip, place, own_o)
    for part in range(groups):
        q_to_partner(None, chip, part, wq.at[pl.ds(part * q_rows, q_rows)])
        o_to_partner(None, chip, place, part, wo.at[pl.ds(part * o_rows, o_rows)])

    stores = [pltpu.make_async_copy(b, a, local.at[k]) for k, (a, b) in enumerate(((q_all.at[tile], v_wq), (o_all.at[tile, place], v_wo)))]
    for load in loads:
        load.wait()
    for store in stores:
        store.start()

    def rows_from_chips(rows):
        for far in range(1, chips):
            for way in (0, 1):
                at = chip - far if way == 0 else chip + far
                for given, row in rows:
                    here = arrives(chip, chips, way, far)
                    here = here if given is None else both(here, given)
                    piece = o_part(at * 2 + core, row, group)
                    arrived(here, piece, ox_s.at[way, far, row], ox_r.at[way, far, row], along_chip(way))
                    if far < chips - 1:
                        o_along_chip(both(here, goes_on(chip, chips, way)), way, far + 1, at, row, piece)
                    o_to_peers(here, at, row, piece)
                    o_to_partner(here, at, row, group, piece)

    def rows_at(far):
        if far == 0:
            return [(None, place)]
        return [(arrives(place, seqs, way, far), place - far if way == 0 else place + far) for way in (0, 1)]

    def out_step(far):
        for way in (0, 1):
            here = arrives(place, seqs, way, far)
            row = place - far if way == 0 else place + far
            piece = o_part(tile, row, group)
            arrived(here, piece, oz_s.at[way, far], oz_r.at[way, far], along_seq(way))
            if far < seqs - 1:
                start(both(here, goes_on(place, seqs, way)), piece, piece, oz_s.at[way, far + 1], oz_r.at[way, far + 1], along_seq(way))
            for side in (0, 1):
                o_along_chip(both(here, goes_on(chip, chips, side)), side, 1, chip, row, piece)
            o_to_peers(here, chip, row, piece)
            o_to_partner(here, chip, row, group, piece)

    def norm_step(far):
        for way in (0, 1):
            here = arrives(place, seqs, way, far)
            row = place - far if way == 0 else place + far
            piece = n_all.at[row]
            arrived(here, piece, nz_s.at[way, far], nz_r.at[way, far], along_seq(way))
            if far < seqs - 1:
                start(both(here, goes_on(place, seqs, way)), piece, piece, nz_s.at[way, far + 1], nz_r.at[way, far + 1], along_seq(way))

    def chip_step(far):
        for way in (0, 1):
            here = arrives(chip, chips, way, far)
            at = chip - far if way == 0 else chip + far
            piece = q_part(at * 2 + core, group)
            arrived(here, piece, qx_s.at[way, far], qx_r.at[way, far], along_chip(way))
            if far < chips - 1:
                start(both(here, goes_on(chip, chips, way)), piece, piece, qx_s.at[way, far + 1], qx_r.at[way, far + 1], along_chip(way))
            q_to_peers(here, at, piece)
            q_to_partner(here, at, group, piece)

    def q_from_peers():
        for step in range(1, groups):
            part = (group + groups - step) % groups
            for at in range(chips):
                away = chip != at
                piece = q_part(at * 2 + core, part)
                arrived(away, piece, qy_s.at[at, step], qy_r.at[at, step], partner)
                q_to_partner(away, at, part, piece)

    def o_from_peers():
        for step in range(1, groups):
            part = (group + groups - step) % groups
            for at in range(chips):
                for row in range(seqs):
                    away = jnp.logical_or(chip != at, place != row)
                    piece = o_part(at * 2 + core, row, part)
                    arrived(away, piece, oy_s.at[at, row, step], oy_r.at[at, row, step], partner)
                    o_to_partner(away, at, row, part, piece)

    last = max(chips, seqs) - 1
    for far in range(1, last + 1):
        if 1 < far < seqs:
            rows_from_chips(rows_at(far - 1))
        if far < seqs:
            norm_step(far)
        if far < seqs - 1:
            out_step(far)
        if far < chips:
            chip_step(far)
        if far == 1 and seqs > 1:
            rows_from_chips(rows_at(0))
        if far == max(chips - 1, min(2, last)):
            q_from_peers()
    for at in range(chips):
        for part in range(groups):
            arrived(None, q_part(at * 2 + other, part), qc_s.at[at, part], qc_r.at[at, part], partner)
    for store in stores:
        store.wait()

    heads = wq.shape[1] // (3 * HD)
    depth, block = wq.shape[0], norm.shape[0]

    def fetch(head):
        slot = head % 2
        columns = pl.ds(pl.multiple_of(head * (3 * HD), 128), 3 * HD)
        return [
            pltpu.make_async_copy(
                q_all.at[at, :, columns], w_head.at[slot, pl.ds(at * depth, depth)], w_sem.at[slot, at]
            )
            for at in range(2 * chips)
        ]

    def one_head(head, carry):
        for load in fetch(head):
            load.wait()

        @pl.when(head + 1 < heads)
        def _():
            for load in fetch(head + 1):
                load.start()

        weights = w_head.at[head % 2]
        for row in range(seqs):
            at = pl.ds(row * block, block)
            part = jnp.dot(n_all[row], weights[...], preferred_element_type=jnp.float32)
            queries[at, :] = root_norm(part[:, :HD]).astype(jnp.bfloat16)
            keys[at, :] = root_norm(part[:, HD : 2 * HD]).astype(jnp.bfloat16)
            values[at, :] = part[:, 2 * HD :].astype(jnp.bfloat16)
        for row in range(seqs):
            at = pl.ds(row * block, block)
            scores = lax.dot_general(
                queries[at, :], keys[...], (((1,), (1,)), ((), ())), preferred_element_type=jnp.float32
            )
            expo = jnp.exp(scores * scale)
            probs = (expo * (1.0 / jnp.sum(expo, axis=-1, keepdims=True))).astype(jnp.bfloat16)
            attended[at, pl.ds(pl.multiple_of(head * HD, 128), HD)] = jnp.dot(
                probs, values[...], preferred_element_type=jnp.float32
            ).astype(jnp.bfloat16)
        return carry

    def between(step):
        if step == 0 and seqs > 1:
            out_step(seqs - 1)
        if step == 1:
            rows_from_chips(rows_at(seqs - 1))
        if step == 2:
            o_from_peers()

    for load in fetch(0):
        load.start()
    cuts = [0, heads // 3, heads // 2, 5 * heads // 6, heads]
    for step in range(4):
        if cuts[step] < cuts[step + 1]:
            lax.fori_loop(cuts[step], cuts[step + 1], one_head, 0)
        between(step)

    for at in range(chips):
        for part in range(groups):
            for row in range(seqs):
                arrived(None, o_part(at * 2 + other, row, part), oc_s.at[at, row, part], oc_r.at[at, row, part], partner)
    for cond, made in sent:
        run(cond, lambda made=made: copy(*made).wait_send())


def gather(norm, wq, wo):
    groups, tiles, seqs = (lax.axis_size(name) for name in ("group", "tile", "seq"))
    chips = tiles // 2
    length = seqs * norm.shape[0]
    pairs = [(2, seqs), (2, seqs), (2, chips), (2, chips, seqs), (chips, groups), (chips, seqs, groups), (chips, groups), (chips, seqs, groups)]
    return pl.pallas_call(
        functools.partial(gather_kernel, groups, chips, seqs, 1.0 / math.sqrt(HD)),
        out_shape=(
            jax.ShapeDtypeStruct((tiles,) + wq.shape, wq.dtype),
            jax.ShapeDtypeStruct((tiles, seqs) + wo.shape, wo.dtype),
            jax.ShapeDtypeStruct((length, wq.shape[1] // 3), norm.dtype),
        ),
        in_specs=[pl.BlockSpec(memory_space=pl.ANY)] * 3,
        out_specs=(pl.BlockSpec(memory_space=pl.ANY),) * 2 + (pl.BlockSpec(memory_space=pltpu.VMEM),),
        scratch_shapes=[pltpu.VMEM((seqs,) + norm.shape, norm.dtype)]
        + [pltpu.VMEM(a.shape, a.dtype) for a in (wq, wo)]
        + [pltpu.VMEM((2, tiles * wq.shape[0], 3 * HD), wq.dtype)]
        + [pltpu.VMEM((length, HD), norm.dtype)] * 3
        + [pltpu.SemaphoreType.DMA((3,)), pltpu.SemaphoreType.DMA((2, tiles))]
        + [pltpu.SemaphoreType.DMA(shape) for shape in pairs for _ in range(2)],
        compiler_params=pltpu.CompilerParams(collective_id=0, has_side_effects=True),
    )(norm, wq, wo)


def tail_kernel(attended, blocks, hidden, modulation, w_head, velocity, summed):
    at = pl.program_id(0)
    width = blocks.shape[2]
    here = pl.ds(pl.multiple_of(at * width, 128), width)
    summed[:, here] = jnp.dot(attended[...], blocks[0], preferred_element_type=jnp.float32)

    @pl.when(at == pl.num_programs(0) - 1)
    def _():
        mixed = hidden[...].astype(jnp.float32) + modulation[2:3] * summed[...]
        norm_out = (layer_norm(mixed) * (1.0 + modulation[4:5]) + modulation[3:4]).astype(jnp.bfloat16)
        velocity[...] = jnp.dot(norm_out, w_head[...], preferred_element_type=jnp.float32)


def tail(attended, blocks, hidden, modulation, w_head):
    tiles, depth, width = blocks.shape
    if width % 128:
        summed = jnp.concatenate(
            [jnp.dot(attended, blocks[at], preferred_element_type=jnp.float32) for at in range(tiles)], axis=1
        )
        mixed = hidden.astype(jnp.float32) + modulation[2] * summed
        norm_out = (layer_norm(mixed) * (1.0 + modulation[4]) + modulation[3]).astype(jnp.bfloat16)
        return jnp.dot(norm_out, w_head, preferred_element_type=jnp.float32)
    whole = [pl.BlockSpec(a.shape, lambda at: (0, 0), pipeline_mode=pl.Buffered(1)) for a in (attended, hidden, modulation, w_head)]
    return pl.pallas_call(
        tail_kernel,
        grid=(tiles,),
        out_shape=jax.ShapeDtypeStruct((hidden.shape[0], w_head.shape[1]), jnp.float32),
        in_specs=[whole[0], pl.BlockSpec((1, depth, width), lambda at: (at, 0, 0)), *whole[1:]],
        out_specs=pl.BlockSpec((hidden.shape[0], w_head.shape[1]), lambda at: (0, 0)),
        scratch_shapes=[pltpu.VMEM(hidden.shape, jnp.float32)],
    )(attended, blocks, hidden, modulation, w_head)


def shards(hidden, modulation, w_qkv, w_out, w_head, latent, weights_int, step_index):
    local = hidden[0].astype(jnp.float32)
    norm_in = (layer_norm(local) * (1.0 + modulation[1]) + modulation[0]).astype(jnp.bfloat16)
    _, out_blocks, attended = gather(norm_in, w_qkv, w_out)
    attended = lax.all_to_all(attended, "seq", split_axis=0, concat_axis=1, tiled=True)
    out_blocks = out_blocks.reshape(out_blocks.shape[0], -1, out_blocks.shape[3])
    velocity = tail(attended, out_blocks, hidden[0], modulation, w_head)
    index = step_index[0].astype(jnp.float32)
    now = noise_level(index, NSTEPS)
    after = noise_level(index + 1.0, NSTEPS)
    base = latent[0]
    weight = weights_int[0].astype(jnp.float32)
    moved = base + (after - now) * velocity
    guess = base - now * velocity
    weighted = jnp.concatenate([moved, guess], axis=1) * weight[:, None]
    seq_count, tile_count = lax.axis_size("seq"), lax.axis_size("tile")
    jump = seq_count - 2
    moves = [
        (t * seq_count + s, (t + 1) * seq_count + s - jump)
        for t in range(tile_count - 1)
        for s in range(jump, seq_count)
    ]
    moves = moves + [(there, here) for here, there in moves]
    other_sums = lax.ppermute(weighted.astype(jnp.bfloat16), ("tile", "seq"), moves)
    other_weight = lax.ppermute(weight.astype(jnp.bfloat16), ("tile", "seq"), moves)
    totals = weighted + other_sums.astype(jnp.float32)
    norms = weight + other_weight.astype(jnp.float32)
    joined = totals / norms[:, None]
    channels = velocity.shape[1]
    return (joined[None, :, :channels], joined[None, :, channels:])


def solution(mesh):
    in_specs = (
        P(("group", "tile"), "seq", None),
        P("group", None),
        P("tile", "seq"),
        P("seq", "tile"),
        P(),
        P(("group", "tile"), "seq", None),
        P(("group", "tile"), "seq"),
        P("group"),
    )
    out_specs = (P(("group", "tile"), "seq", None), P(("group", "tile"), "seq", None))
    return jax.shard_map(shards, mesh=mesh, in_specs=in_specs, out_specs=out_specs, check_vma=False)
```

profile of v0, /device:TPU:2, one launch (start us, length us, event | category | flops | bytes accessed | tf_op | source)
XLA Modules:
  0.0 261.0 jit_solution(18182251112621841405)
XLA Ops:
  0.6 0.0 copy-start
  0.6 1.1 slice_add_fusion
  1.7 1.7 convert_reduce_fusion
  3.4 2.0 fusion.2
  5.4 1.9 fusion.5.norm
  7.3 186.6 %shard_map.95 = (bf16[4,768,2304]{2,1,0:T(8,128)(2,1)}, bf16[4,4,768,768]{3,2,1,0:T(8,128)(2,1)}, bf16[1024,768]{1,0:T(8,128)(2,1)}) custom-call(bf16[256,3072]{1,0:T(8,128)(2,1)} %fusion.5.norm, bf16[768,2304]{1,0:T(8,128)(2,1)} %wq.1, bf16[768,768]{1,0:T(8,128)(2,1)} %wo.1), custom_call_target="tpu_custom_call" | custom-call | tf_op jit(solution)/shard_map/pallas_call | solution.py:300
  194.0 0.0 copy-start.3
  194.0 0.0 copy-start.1
  194.0 0.0 copy-start.2
  194.0 5.3 %all-to-all-start = ((bf16[4,256,768]{2,1,0:T(8,128)(2,1)}), bf16[4,256,768]{2,1,0:T(8,128)(2,1)S(1)}, u32[]{:S(2)}, u32[]{:S(2)}) async-start(bf16[4,256,768]{2,1,0:T(8,128)(2,1)} %bitcast.25), calls=%async_computation | async-start | bytes 3145728 | tf_op jit(solution)/shard_map/all_to_all | solution.py:356
  199.3 1.9 collective-permute-start.1
  201.9 1.2 copy.17.w_head
  203.0 0.1 copy.15
  203.2 33.7 %all-to-all-done = bf16[4,256,768]{2,1,0:T(8,128)(2,1)S(1)} async-done(((bf16[4,256,768]{2,1,0:T(8,128)(2,1)}), bf16[4,256,768]{2,1,0:T(8,128)(2,1)S(1)}, u32[]{:S(2)}, u32[]{:S(2)}) %all-to-all-start) | async-done | bytes 1572896 | tf_op jit(solution)/shard_map/all_to_all | solution.py:356
  236.9 1.4 copy.20
  238.3 12.5 %shard_map.96 = f32[256,64]{1,0:T(8,128)} custom-call(bf16[256,3072]{1,0:T(8,128)(2,1)} %bitcast.24, bf16[4,3072,768]{2,1,0:T(8,128)(2,1)} %bitcast.22, bf16[256,3072]{1,0:T(8,128)(2,1)} %bitcast.21, f32[5,3072]{1,0:T(8,128)} %modulation.1, bf16[3072,64]{1,0:T(8,128)(2,1)} %copy.17.w_head), custom_call_target="tpu_custom_call" | custom-call | tf_op jit(solution)/shard_map/pallas_call | solution.py:342
  250.8 0.9 bitcast_add_fusion
  251.7 0.1 fusion.6
  251.9 1.9 collective-permute-start
  253.8 5.4 %collective-permute-done = bf16[256,128]{1,0:T(8,128)(2,1)S(1)} collective-permute-done((bf16[256,128]{1,0:T(8,128)(2,1)S(1)}, bf16[256,128]{1,0:T(8,128)(2,1)S(1)}, u32[]{:S(2)}, u32[]{:S(2)}) %collective-permute-start) | collective-permute-done | bytes 65568 | tf_op jit(solution)/shard_map/ppermute | solution.py:375
  259.3 0.2 add_divide_fusion
  259.4 0.1 slice_bitcast_fusion
  259.5 0.7 copy.18
  260.3 0.7 copy.19
  (10 shorter events, 0.0 us)
Async XLA Ops:
  0.6 4.8 %copy-start = (bf16[1,256,3072]{2,1,0:T(8,128)(2,1)S(1)}, bf16[1,256,3072]{2,1,0:T(8,128)(2,1)}, u32[]{:S(2)}) copy-start(bf16[1,256,3072]{2,1,0:T(8,128)(2,1)} %param.8) | copy-start | bytes 4718596
  194.0 5.3 %copy-start.3 = (s32[1,256]{1,0:T(1,128)S(1)}, s32[1,256]{1,0:T(1,128)}, u32[]{:S(2)}) copy-start(s32[1,256]{1,0:T(1,128)} %param.14) | copy-start | bytes 3076
  194.0 7.9 %copy-start.1 = (bf16[3072,64]{0,1:T(8,128)(2,1)S(1)}, bf16[3072,64]{0,1:T(8,128)(2,1)}, u32[]{:S(2)}) copy-start(bf16[3072,64]{0,1:T(8,128)(2,1)} %param.12) | copy-start | bytes 1179652
  194.0 9.0 %copy-start.2 = (f32[1,256,64]{1,2,0:T(8,128)S(1)}, f32[1,256,64]{1,2,0:T(8,128)}, u32[]{:S(2)}) copy-start(f32[1,256,64]{1,2,0:T(8,128)} %param.13) | copy-start | bytes 196612
  194.0 42.9 %all-to-all-start = ((bf16[4,256,768]{2,1,0:T(8,128)(2,1)}), bf16[4,256,768]{2,1,0:T(8,128)(2,1)S(1)}, u32[]{:S(2)}, u32[]{:S(2)}) async-start(bf16[4,256,768]{2,1,0:T(8,128)(2,1)} %bitcast.25), calls=%async_computation | async-start | bytes 3145728 | tf_op jit(solution)/shard_map/all_to_all | solution.py:356
  199.3 54.5 %collective-permute-start.1 = (bf16[256]{0:T(256)(128)(2,1)S(1)}, bf16[256]{0:T(256)(128)(2,1)S(1)}, u32[]{:S(2)}, u32[]{:S(2)}) collective-permute-start(bf16[256]{0:T(256)(128)(2,1)S(1)} %convert_element_type.39), channel_id=1, source_target_pairs={{2,4},{3,5},{6,8},{7,9},{10,12},{11,13},{4,2},{5,3},{8,6},{9,7},{1... | collective-permute-start | bytes 1544 | tf_op jit(solution)/shard_map/ppermute | solution.py:376
  251.9 7.4 %collective-permute-start = (bf16[256,128]{1,0:T(8,128)(2,1)S(1)}, bf16[256,128]{1,0:T(8,128)(2,1)S(1)}, u32[]{:S(2)}, u32[]{:S(2)}) collective-permute-start(bf16[256,128]{1,0:T(8,128)(2,1)S(1)} %fusion.6), channel_id=1, source_target_pairs={{2,4},{3,5},{6,8},{7,9},{10,12},{11,13},{4,2},{5,3},{8,6},{9,7},{1... | collective-permute-start | bytes 196616 | tf_op jit(solution)/shard_map/ppermute | solution.py:375
where the time goes:
time: 261 us
  Pallas kernels  199 us (76%)
  waiting for transfers between devices  39.1 us (15%)
  starting transfers between devices  9.1 us (3%)
  other arithmetic  7.93 us (3%)
  local copies, waits for them, and re-layouts  4.17 us (2%)
    pallas_call x1, Pallas kernels, gather(): pl.pallas_call(functools.partial(gather_kernel, groups, chips, seqs, 1.0...  187 us
    all_to_all x1, waiting for transfers between devices, shards(): lax.all_to_all(attended, 'seq', split_axis=0, concat_axis=1, tiled=True)  33.7 us
    pallas_call x1, Pallas kernels, tail(): pl.pallas_call(tail_kernel, grid=(tiles,), out_shape=jax.ShapeDtypeStruct...  12.5 us
    ppermute x1, waiting for transfers between devices, shards(): lax.ppermute(weighted.astype(jnp.bfloat16), ('tile', 'seq'), moves)  5.43 us
    all_to_all x1, starting transfers between devices, shards(): lax.all_to_all(attended, 'seq', split_axis=0, concat_axis=1, tiled=True)  5.26 us
  transfers between devices with their start and end apart: 3, of which 2 were waited for; matrix products, arithmetic and copies ran while one was open for 1% of the time, Pallas kernels for 5%

commit v1 on v0

--- a/solution.py
+++ b/solution.py
@@ -349,21 +349,419 @@
     )(attended, blocks, hidden, modulation, w_head)
 
 
-def shards(hidden, modulation, w_qkv, w_out, w_head, latent, weights_int, step_index):
+def step_kernel(
+    scale, hidden, wq, wo, modulation, w_head, velocity,
+    n_all, normed, w_all, queries, keys, values, attended, att_in, o_all, summed, vel, vel_in, local,
+    nz_s, nz_r, qx_s, qx_r, qy_s, qy_r, qc_s, qc_r, qo_s, qo_r, oz_s, oz_r, ox_s, ox_r, oy_s, oy_r, oc_s, oc_r,
+    at_s, at_r, vl_s, vl_r,
+):
+    group, tile, place = lax.axis_index("group"), lax.axis_index("tile"), lax.axis_index("seq")
+    seqs, block, width = n_all.shape
+    chip, core = tile // 2, tile % 2
+    side = place // 2
+    toward = 1 - 2 * side
+    inner = jnp.logical_or(place == 1, place == 2)
+    outer_end = jnp.logical_not(inner)
+    over = (1 - chip) * 2 + core
+    mate = chip * 2 + 1 - core
+    mate_over = (1 - chip) * 2 + 1 - core
+    x_dev, y_dev, p_dev, in_dev = {"tile": over}, {"group": 1 - group}, {"tile": mate}, {"seq": place + toward}
+    out_dev = {"seq": place - toward}
+    depth, cols = wq.shape
+    q_half, o_half = depth // 2, wo.shape[0] // 2
+    chunks = qx_s.shape[0]
+    piece = q_half // chunks
+    pairs = attended.shape[0]
+    heads = queries.shape[0]
+    both = jnp.logical_and
+
+    def yes():
+        return None
+
+    def middle():
+        return inner
+
+    def ends():
+        return outer_end
+
+    def along(way):
+        return {"seq": place + 1 - 2 * way}
+
+    barrier = pltpu.get_barrier_semaphore()
+    greet = [x_dev, y_dev, p_dev] + [{"seq": (place + far) % seqs} for far in range(1, seqs)]
+    for device in greet:
+        pl.semaphore_signal(barrier, inc=1, device_id=device, device_id_type=MESH)
+    pl.semaphore_wait(barrier, len(greet))
+
+    sent = []
+
+    def copy(source, target, send, recv, device):
+        return pltpu.make_async_remote_copy(
+            src_ref=source, dst_ref=target, send_sem=send, recv_sem=recv, device_id=device, device_id_type=MESH
+        )
+
+    def start(cond, make):
+        run(cond(), lambda: copy(*make()).start())
+        sent.append((cond, make))
+
+    def arrived(cond, target, recv):
+        run(cond, lambda: copy(target(), target(), recv, recv, p_dev).wait_recv())
+
+    def w_rows(owner, part, at):
+        return w_all.at[pl.ds(pl.multiple_of(owner * depth + part * q_half + at * piece, 16), piece)]
+
+    def w_block(owner):
+        return w_all.at[pl.ds(pl.multiple_of(owner * depth, 16), depth)]
+
+    def o_rows(owner, kind, part):
+        return o_all.at[owner, kind, pl.ds(pl.multiple_of(part * o_half, 16), o_half)]
+
+    loads = [pltpu.make_async_copy(a, b, local.at[k]) for k, (a, b) in enumerate(((hidden, n_all.at[place]), (wq, w_block(tile))))]
+    load_o = pltpu.make_async_copy(wo, o_all.at[tile, 0], local.at[2])
+    for way in (0, 1):
+        start(lambda way=way: goes_on(place, seqs, way), lambda way=way: (hidden, n_all.at[place], nz_s.at[way, 1], nz_r.at[way, 1], along(way)))
+    for at in range(chunks):
+        start(yes, lambda at=at: (
+            wq.at[pl.ds(pl.multiple_of(group * q_half + at * piece, 16), piece)], w_rows(tile, group, at),
+            qx_s.at[at], qx_r.at[at], x_dev))
+    for load in loads:
+        load.start()
+    start(yes, lambda: (wq, w_block(tile), qo_s, qo_r, p_dev))
+    start(middle, lambda: (wo, o_all.at[tile, 0], ox_s.at[0], ox_r.at[0], x_dev))
+    run(inner, load_o.start)
+    start(middle, lambda: (wo, o_all.at[tile, 0], oc_s.at[0, 0], oc_r.at[0, 0], p_dev))
+
+    values[:, :, HD:] = jnp.ones((heads, values.shape[1], HD), values.dtype)
+
+    def tokens(far):
+        for way in (0, 1):
+            here = arrives(place, seqs, way, far)
+            row = functools.partial(lambda way: place - far if way == 0 else place + far, way)
+            arrived(here, lambda row=row: n_all.at[row()], nz_r.at[way, far])
+            if far < seqs - 1:
+                start(
+                    lambda way=way: both(arrives(place, seqs, way, far), goes_on(place, seqs, way)),
+                    lambda row=row, way=way: (
+                        n_all.at[row()], n_all.at[row()], nz_s.at[way, far + 1], nz_r.at[way, far + 1], along(way)))
+
+    def q_over(at):
+        arrived(None, lambda: w_rows(over, group, at), qx_r.at[at])
+        start(yes, lambda: (w_rows(over, group, at), w_rows(over, group, at), qy_s.at[at], qy_r.at[at], y_dev))
+        start(yes, lambda: (w_rows(over, group, at), w_rows(over, group, at), qc_s.at[0, at], qc_r.at[group, at], p_dev))
+
+    def q_peer(at):
+        arrived(None, lambda: w_rows(over, 1 - group, at), qy_r.at[at])
+        start(yes, lambda: (
+            w_rows(over, 1 - group, at), w_rows(over, 1 - group, at), qc_s.at[1, at], qc_r.at[1 - group, at], p_dev))
+
+    def o_first():
+        start(ends, lambda: (
+            wo.at[pl.ds(pl.multiple_of(group * o_half, 16), o_half)], o_rows(tile, 2, group), oz_s.at[0], oz_r.at[2], in_dev))
+        start(middle, lambda: (
+            wo.at[pl.ds(pl.multiple_of(group * o_half, 16), o_half)], o_rows(tile, 1, group), oz_s.at[1], oz_r.at[1], in_dev))
+
+    def o_chain(kind):
+        arrived(inner, lambda: o_rows(tile, kind, group), oz_r.at[kind])
+        if kind == 2:
+            start(middle, lambda: (o_rows(tile, 2, group), o_rows(tile, 3, group), oz_s.at[2], oz_r.at[3], in_dev))
+        start(middle, lambda: (o_rows(tile, kind, group), o_rows(tile, kind, group), ox_s.at[kind], ox_r.at[kind], x_dev))
+        start(middle, lambda: (o_rows(tile, kind, group), o_rows(tile, kind, group), oy_s.at[0, kind], oy_r.at[0, kind], y_dev))
+
+    def o_over(kind):
+        if kind == 0:
+            arrived(inner, lambda: o_all.at[over, 0], ox_r.at[0])
+            start(middle, lambda: (o_all.at[over, 0], o_all.at[over, 0], oc_s.at[1, 0], oc_r.at[1, 0], p_dev))
+        else:
+            arrived(inner, lambda: o_rows(over, kind, group), ox_r.at[kind])
+            start(middle, lambda: (
+                o_rows(over, kind, group), o_rows(over, kind, group), oy_s.at[1, kind], oy_r.at[1, kind], y_dev))
+
+    def o_peer(which, kind):
+        owner = tile if which == 0 else over
+        arrived(inner, lambda: o_rows(owner, kind, 1 - group), oy_r.at[which, kind])
+        start(middle, lambda: (
+            o_all.at[owner, kind], o_all.at[owner, kind], oc_s.at[which, kind], oc_r.at[which, kind], p_dev))
+
+    q_over(0)
+    for at in range(1, chunks):
+        if at == chunks - 1:
+            tokens(1)
+            o_first()
+        q_over(at)
+        q_peer(at - 1)
+    q_peer(chunks - 1)
+    for load in loads:
+        load.wait()
+    arrived(None, lambda: w_block(mate), qo_r)
+    for part in (0, 1):
+        for at in range(chunks):
+            arrived(None, lambda: w_rows(mate_over, part, at), qc_r.at[part, at])
+
+    strip = 32
+
+    def project(row):
+        def norm(at, carry):
+            rows = pl.ds(pl.multiple_of(at * strip, strip), strip)
+            given = n_all[row, rows, :].astype(jnp.float32)
+            normed[rows, :] = (layer_norm(given) * (1.0 + modulation[1:2]) + modulation[0:1]).astype(normed.dtype)
+            return carry
+
+        lax.fori_loop(0, block // strip, norm, 0)
+        place_of = pl.ds(pl.multiple_of(row * block, block), block)
+
+        def one(pair, carry):
+            part = jnp.dot(
+                normed[...], w_all[:, pl.ds(pl.multiple_of(pair * (6 * HD), 128), 6 * HD)], preferred_element_type=jnp.float32
+            )
+            for at in (0, 1):
+                here = 3 * HD * at
+                queries[2 * pair + at, place_of, :] = root_norm(part[:, here : here + HD]).astype(queries.dtype)
+                keys[2 * pair + at, place_of, :] = root_norm(part[:, here + HD : here + 2 * HD]).astype(keys.dtype)
+                values[2 * pair + at, place_of, pl.ds(0, HD)] = part[:, here + 2 * HD : here + 3 * HD].astype(values.dtype)
+            return carry
+
+        lax.fori_loop(0, pairs, one, 0)
+
+    def in_order(step, carry):
+        @pl.when(step == 1)
+        def _():
+            o_chain(2)
+
+        @pl.when(step == 3)
+        def _():
+            tokens(2)
+
+        @pl.when(step == 5)
+        def _():
+            o_over(0)
+            o_peer(0, 2)
+            o_over(2)
+            o_chain(1)
+            tokens(3)
+
+        far, way = (step + 1) // 2, (step + 1) % 2
+        row = place + far * (2 * way - 1)
+
+        @pl.when(both(row >= 0, row < seqs))
+        def _():
+            project(row)
+
+        return carry
+
+    lax.fori_loop(0, 2 * seqs - 1, in_order, 0)
+
+    def slot_of(row):
+        return row // 2 + 1, 0 if row in (1, 2) else 1
+
+    def kind_at(target):
+        return 2 * outer_end.astype(jnp.int32) + (side != target // 2).astype(jnp.int32)
+
+    def leave(pair, row):
+        target, slot = slot_of(row)
+        kind = kind_at(target)
+        source = attended.at[pair, pl.ds(row * block, block)]
+        landing = att_in.at[kind, pair, pl.ds(slot * block, block)]
+        away = copy(source, landing, at_s.at[row, pair], at_r.at[kind, slot, pair], {"seq": target})
+        stay = pltpu.make_async_copy(source, landing, at_r.at[kind, slot, pair])
+        return place != target, away, place == target, stay
+
+    def one_head(head, carry):
+        pair = head // 2
+        lanes = pl.ds(pl.multiple_of((head % 2) * HD, HD), HD)
+        for row in range(seqs):
+            at = pl.ds(row * block, block)
+            scores = lax.dot_general(
+                queries[head, at, :], keys[head], (((1,), (1,)), ((), ())), preferred_element_type=jnp.float32
+            )
+            expo = jnp.exp2(scores * scale).astype(jnp.bfloat16)
+            mixed = jnp.dot(expo, values[head], preferred_element_type=jnp.float32)
+            attended[pair, at, lanes] = (mixed[:, :HD] * (1.0 / mixed[:, HD:])).astype(attended.dtype)
+
+        @pl.when(head % 2 == 1)
+        def _():
+            for row in range(seqs):
+                far, away, near, stay = leave(pair, row)
+                run(far, away.start)
+                run(near, stay.start)
+
+        @pl.when(head == 1)
+        def _():
+            o_peer(1, 2)
+
+        @pl.when(head == heads // 2)
+        def _():
+            o_chain(3)
+            o_over(1)
+
+        @pl.when(head == heads - 1)
+        def _():
+            o_peer(0, 1)
+            o_over(3)
+
+        return carry
+
+    lax.fori_loop(0, heads, one_head, 0)
+
+    @pl.when(inner)
+    def _():
+        summed[...] = jnp.zeros_like(summed)
+
+    run(inner, load_o.wait)
+
+    def accumulate(kind, carry):
+        @pl.when(kind == 1)
+        def _():
+            o_peer(1, 1)
+
+        @pl.when(kind == 3)
+        def _():
+            o_peer(0, 3)
+            o_peer(1, 3)
+
+        @pl.when(inner)
+        def _():
+            copy(o_all.at[mate, kind], o_all.at[mate, kind], oc_s.at[0, kind], oc_r.at[0, kind], p_dev).wait_recv()
+            copy(o_all.at[mate_over, kind], o_all.at[mate_over, kind], oc_s.at[1, kind], oc_r.at[1, kind], p_dev).wait_recv()
+
+            for slot in (0, 1):
+                for pair in range(pairs):
+                    landing = att_in.at[kind, pair, pl.ds(slot * block, block)]
+                    source = attended.at[pair, pl.ds(0, block)]
+                    got = at_r.at[kind, slot, pair]
+
+                    @pl.when(kind == 0)
+                    def _():
+                        pltpu.make_async_copy(source, landing, got).wait()
+
+                    @pl.when(kind != 0)
+                    def _():
+                        copy(landing, landing, got, got, p_dev).wait_recv()
+
+            def columns(owner, carry):
+                here = pl.ds(pl.multiple_of(owner * wo.shape[1], 128), wo.shape[1])
+                total = summed[:, here]
+                for pair in range(pairs):
+                    total += jnp.dot(
+                        att_in[kind, pair], o_all[owner, kind, pl.ds(pair * 2 * HD, 2 * HD), :],
+                        preferred_element_type=jnp.float32,
+                    )
+                summed[:, here] = total
+                return carry
+
+            lax.fori_loop(0, o_all.shape[0], columns, 0)
+
+        return carry
+
+    lax.fori_loop(0, seqs, accumulate, 0)
+
+    def send_vel():
+        return copy(vel.at[1], vel_in, vl_s, vl_r, out_dev)
+
+    @pl.when(inner)
+    def _():
+        def finish(step, carry):
+            slot = 1 - step
+            row = place - toward * slot
+
+            def norm(at, carry):
+                rows = pl.ds(pl.multiple_of(at * strip, strip), strip)
+                sums = pl.ds(pl.multiple_of(slot * block + at * strip, strip), strip)
+                mixed = n_all[row, rows, :].astype(jnp.float32) + modulation[2:3] * summed[sums, :]
+                normed[rows, :] = (layer_norm(mixed) * (1.0 + modulation[4:5]) + modulation[3:4]).astype(normed.dtype)
+                return carry
+
+            lax.fori_loop(0, block // strip, norm, 0)
+            vel[slot] = lax.dot_general(
+                w_head[...], normed[...], (((1,), (1,)), ((), ())), preferred_element_type=jnp.float32
+            )
+
+            @pl.when(slot == 1)
+            def _():
+                send_vel().start()
+
+            return carry
+
+        lax.fori_loop(0, 2, finish, 0)
+        velocity[...] = vel[0]
+        send_vel().wait_send()
+
+    @pl.when(outer_end)
+    def _():
+        copy(vel_in, vel_in, vl_s, vl_r, p_dev).wait_recv()
+        velocity[...] = vel_in[...]
+
+    def drain(pair, carry):
+        for row in range(seqs):
+            far, away, _, _ = leave(pair, row)
+            run(far, away.wait_send)
+        return carry
+
+    lax.fori_loop(0, pairs, drain, 0)
+    for cond, make in sent:
+        run(cond(), lambda make=make: copy(*make()).wait_send())
+
+
+def fused(hidden, wq, wo, modulation, w_head):
+    tiles, seqs = lax.axis_size("tile"), lax.axis_size("seq")
+    block, width = hidden.shape
+    length, heads = seqs * block, wq.shape[1] // (3 * HD)
+    pairs, chunks = heads // 2, 3
+    sizes = [(2, seqs)] * 2 + [(chunks,)] * 4 + [(2, chunks)] * 2 + [()] * 2 + [(3,), (4,)] + [(4,)] * 2 + [(2, 4)] * 4
+    sizes += [(seqs, pairs), (4, 2, pairs), (), ()]
+    any_space, vmem = pl.BlockSpec(memory_space=pl.ANY), pl.BlockSpec(memory_space=pltpu.VMEM)
+    return pl.pallas_call(
+        functools.partial(step_kernel, math.log2(math.e) / math.sqrt(HD)),
+        out_shape=jax.ShapeDtypeStruct((w_head.shape[0], block), jnp.float32),
+        in_specs=[any_space] * 3 + [vmem] * 2,
+        out_specs=vmem,
+        scratch_shapes=[
+            pltpu.VMEM((seqs, block, width), hidden.dtype),
+            pltpu.VMEM((block, width), hidden.dtype),
+            pltpu.VMEM((tiles * wq.shape[0], wq.shape[1]), wq.dtype),
+            pltpu.VMEM((heads, length, HD), hidden.dtype),
+            pltpu.VMEM((heads, length, HD), hidden.dtype),
+            pltpu.VMEM((heads, length, 2 * HD), hidden.dtype),
+            pltpu.VMEM((pairs, length, 2 * HD), hidden.dtype),
+            pltpu.VMEM((4, pairs, 2 * block, 2 * HD), hidden.dtype),
+            pltpu.VMEM((tiles, 4) + wo.shape, wo.dtype),
+            pltpu.VMEM((2 * block, width), jnp.float32),
+            pltpu.VMEM((2, w_head.shape[0], block), jnp.float32),
+            pltpu.VMEM((w_head.shape[0], block), jnp.float32),
+            pltpu.SemaphoreType.DMA((3,)),
+        ]
+        + [pltpu.SemaphoreType.DMA(shape) for shape in sizes],
+        compiler_params=pltpu.CompilerParams(collective_id=1, has_side_effects=True, vmem_limit_bytes=67043328),
+    )(hidden, wq, wo, modulation, w_head)
+
+
+def fits(hidden, w_qkv, w_out):
+    sizes = tuple(lax.axis_size(name) for name in ("group", "tile", "seq"))
+    heads = w_qkv.shape[1] // (3 * HD)
+    return sizes == (2, 4, 4) and heads % 2 == 0 and w_out.shape[1] % 128 == 0 and w_qkv.shape[0] % 96 == 0
+
+
+def spread(hidden, modulation, w_qkv, w_out, w_head):
     local = hidden[0].astype(jnp.float32)
     norm_in = (layer_norm(local) * (1.0 + modulation[1]) + modulation[0]).astype(jnp.bfloat16)
     _, out_blocks, attended = gather(norm_in, w_qkv, w_out)
     attended = lax.all_to_all(attended, "seq", split_axis=0, concat_axis=1, tiled=True)
     out_blocks = out_blocks.reshape(out_blocks.shape[0], -1, out_blocks.shape[3])
-    velocity = tail(attended, out_blocks, hidden[0], modulation, w_head)
+    return tail(attended, out_blocks, hidden[0], modulation, w_head)
+
+
+def shards(hidden, modulation, w_qkv, w_out, w_head, latent, weights_int, step_index):
+    if fits(hidden, w_qkv, w_out):
+        velocity = fused(hidden[0], w_qkv, w_out, modulation, w_head.T)
+    else:
+        velocity = spread(hidden, modulation, w_qkv, w_out, w_head).T
     index = step_index[0].astype(jnp.float32)
     now = noise_level(index, NSTEPS)
     after = noise_level(index + 1.0, NSTEPS)
-    base = latent[0]
+    base = latent[0].T
     weight = weights_int[0].astype(jnp.float32)
     moved = base + (after - now) * velocity
     guess = base - now * velocity
-    weighted = jnp.concatenate([moved, guess], axis=1) * weight[:, None]
+    weighted = jnp.concatenate([moved, guess], axis=0) * weight[None, :]
     seq_count, tile_count = lax.axis_size("seq"), lax.axis_size("tile")
     jump = seq_count - 2
     moves = [
@@ -376,9 +774,9 @@
     other_weight = lax.ppermute(weight.astype(jnp.bfloat16), ("tile", "seq"), moves)
     totals = weighted + other_sums.astype(jnp.float32)
     norms = weight + other_weight.astype(jnp.float32)
-    joined = totals / norms[:, None]
-    channels = velocity.shape[1]
-    return (joined[None, :, :channels], joined[None, :, channels:])
+    joined = totals / norms[None, :]
+    channels = velocity.shape[0]
+    return (joined[:channels].T[None], joined[channels:].T[None])
 
 
 def solution(mesh):

time: 261 us -> 198 us (0.76)
  waiting for transfers between devices: 39.1 us -> 3.11 us
  Pallas kernels: 199 us -> 174 us
  starting transfers between devices: 9.1 us -> 12.8 us
  other arithmetic: 7.93 us -> 4.23 us
  local copies, waits for them, and re-layouts: 4.17 us -> 1.22 us
    all_to_all x1 -> x0, waiting for transfers between devices: 33.7 us -> none  [shards(): lax.all_to_all(attended, 'seq', split_axis=0, concat_axis=1, tiled=True)]
    pallas_call x2 -> x1, Pallas kernels: 199 us -> 174 us  [fused(): pl.pallas_call(functools.partial(step_kernel, math.log2(math.e) / math.sq...]
    ppermute x1, starting transfers between devices: 1.92 us -> 8.93 us  [shards(): lax.ppermute(weighted.astype(jnp.bfloat16), ('tile', 'seq'), moves)]
    all_to_all x1 -> x0, starting transfers between devices: 5.26 us -> none  [shards(): lax.all_to_all(attended, 'seq', split_axis=0, concat_axis=1, tiled=True)]
    reduce_sum x2 -> x0, other arithmetic: 3.66 us -> none  [the longest x1 1.96 us: layer_norm(): spread = jnp.mean(centred * centred, axis=-1, keepdims=True)]
  transfers between devices with their start and end apart: 3 -> 2, of which waited for: 2 -> 1; matrix products, arithmetic and copies ran while one was open for 1% -> 1% of each run, Pallas kernels for 5% -> 88%
where the time goes in v1:
time: 198 us; the launch traced here: 196 us
  Pallas kernels  174 us (88%)
  starting transfers between devices  12.8 us (6%)
  other arithmetic  4.23 us (2%)
  waiting for transfers between devices  3.11 us (2%)
    pallas_call x1, Pallas kernels, fused(): pl.pallas_call(functools.partial(step_kernel, math.log2(math.e) / math.sq...  174 us
    ppermute x1, starting transfers between devices, shards(): lax.ppermute(weighted.astype(jnp.bfloat16), ('tile', 'seq'), moves)  8.93 us
  transfers between devices with their start and end apart: 2, of which 1 were waited for; matrix products, arithmetic and copies ran while one was open for 1% of the time, Pallas kernels for 88%

profile of v1, /device:TPU:2, one launch (start us, length us, event | category | flops | bytes accessed | tf_op | source)
XLA Modules:
  0.0 196.4 jit_solution(4116493155750384397)
XLA Ops:
  0.6 0.7 convert_element_type.22
  1.3 0.0 copy-start
  1.3 0.6 copy-done
  1.9 0.6 convert_element_type.25
  2.5 3.9 %collective-permute-start.1 = (bf16[256]{0:T(256)(128)(2,1)}, bf16[256]{0:T(256)(128)(2,1)}, u32[]{:S(2)}, u32[]{:S(2)}) collective-permute-start(bf16[256]{0:T(256)(128)(2,1)} %convert_element_type.25), channel_id=1, source_target_pairs={{2,4},{3,5},{6,8},{7,9},{10,12},{11,13},{4,2},{5,3},{8,6},{9,7},{1... | collective-permute-start | bytes 1544 | tf_op jit(solution)/shard_map/ppermute | solution.py:774
  7.1 173.6 %shard_map.95 = f32[64,256]{1,0:T(8,128)} custom-call(bf16[256,3072]{1,0:T(8,128)(2,1)} %bitcast.18, bf16[768,2304]{1,0:T(8,128)(2,1)} %wq.1, bf16[768,768]{1,0:T(8,128)(2,1)} %wo.1, f32[5,3072]{1,0:T(8,128)} %modulation.1, bf16[64,3072]{1,0:T(8,128)(2,1)} %bitcast.19), custom_call_target="tpu_custom_call" | custom-call | tf_op jit(solution)/shard_map/pallas_call | solution.py:712
  180.7 0.9 bitcast_add_fusion
  181.6 0.7 fusion
  182.3 8.9 %collective-permute-start = (bf16[128,256]{1,0:T(8,128)(2,1)S(1)}, bf16[128,256]{1,0:T(8,128)(2,1)S(1)}, u32[]{:S(2)}, u32[]{:S(2)}) collective-permute-start(bf16[128,256]{1,0:T(8,128)(2,1)S(1)} %fusion), channel_id=1, source_target_pairs={{2,4},{3,5},{6,8},{7,9},{10,12},{11,13},{4,2},{5,3},{8,6},{9,7},{1... | collective-permute-start | bytes 196616 | tf_op jit(solution)/shard_map/ppermute | solution.py:773
  191.3 0.0 collective-permute-done.1
  191.3 0.7 convert_add_fusion
  192.0 3.1 %collective-permute-done = bf16[128,256]{1,0:T(8,128)(2,1)S(1)} collective-permute-done((bf16[128,256]{1,0:T(8,128)(2,1)S(1)}, bf16[128,256]{1,0:T(8,128)(2,1)S(1)}, u32[]{:S(2)}, u32[]{:S(2)}) %collective-permute-start) | collective-permute-done | bytes 65568 | tf_op jit(solution)/shard_map/ppermute | solution.py:773
  195.1 0.7 add_divide_fusion
  195.8 0.7 slice_bitcast_fusion
Async XLA Ops:
  1.3 0.6 copy-start
  2.5 188.8 %collective-permute-start.1 = (bf16[256]{0:T(256)(128)(2,1)}, bf16[256]{0:T(256)(128)(2,1)}, u32[]{:S(2)}, u32[]{:S(2)}) collective-permute-start(bf16[256]{0:T(256)(128)(2,1)} %convert_element_type.25), channel_id=1, source_target_pairs={{2,4},{3,5},{6,8},{7,9},{10,12},{11,13},{4,2},{5,3},{8,6},{9,7},{1... | collective-permute-start | bytes 1544 | tf_op jit(solution)/shard_map/ppermute | solution.py:774
  182.3 12.7 %collective-permute-start = (bf16[128,256]{1,0:T(8,128)(2,1)S(1)}, bf16[128,256]{1,0:T(8,128)(2,1)S(1)}, u32[]{:S(2)}, u32[]{:S(2)}) collective-permute-start(bf16[128,256]{1,0:T(8,128)(2,1)S(1)} %fusion), channel_id=1, source_target_pairs={{2,4},{3,5},{6,8},{7,9},{10,12},{11,13},{4,2},{5,3},{8,6},{9,7},{1... | collective-permute-start | bytes 196616 | tf_op jit(solution)/shard_map/ppermute | solution.py:773

commit v2 on v1

--- a/solution.py
+++ b/solution.py
@@ -350,10 +350,11 @@
 
 
 def step_kernel(
-    scale, hidden, wq, wo, modulation, w_head, velocity,
-    n_all, normed, w_all, queries, keys, values, attended, att_in, o_all, summed, vel, vel_in, local,
+    scale, hidden, wq, wo, modulation, w_head, latent, weight, index, stepped, clean,
+    n_all, normed, w_all, queries, keys, values, attended, att_in, o_all, summed,
+    lat_in, wt_in, joint, msg, msg_in, result, local,
     nz_s, nz_r, qx_s, qx_r, qy_s, qy_r, qc_s, qc_r, qo_s, qo_r, oz_s, oz_r, ox_s, ox_r, oy_s, oy_r, oc_s, oc_r,
-    at_s, at_r, vl_s, vl_r,
+    at_s, at_r, ln_s, ln_r, wt_s, wt_r, ms_s, ms_r, rs_s, rs_r,
 ):
     group, tile, place = lax.axis_index("group"), lax.axis_index("tile"), lax.axis_index("seq")
     seqs, block, width = n_all.shape
@@ -391,7 +392,16 @@
     greet = [x_dev, y_dev, p_dev] + [{"seq": (place + far) % seqs} for far in range(1, seqs)]
     for device in greet:
         pl.semaphore_signal(barrier, inc=1, device_id=device, device_id_type=MESH)
-    pl.semaphore_wait(barrier, len(greet))
+    step_tile = 2 * side - 1
+    tiles = lax.axis_size("tile")
+    paired = jnp.logical_and(inner, jnp.logical_and(tile + step_tile >= 0, tile + step_tile < tiles))
+    j_dev = {"tile": tile + step_tile, "seq": seqs - 1 - place}
+
+    @pl.when(paired)
+    def _():
+        pl.semaphore_signal(barrier, inc=1, device_id=j_dev, device_id_type=MESH)
+
+    pl.semaphore_wait(barrier, len(greet) + paired.astype(jnp.int32))
 
     sent = []
 
@@ -428,6 +438,10 @@
         load.start()
     start(yes, lambda: (wq, w_block(tile), qo_s, qo_r, p_dev))
     start(middle, lambda: (wo, o_all.at[tile, 0], ox_s.at[0], ox_r.at[0], x_dev))
+    start(ends, lambda: (wo, o_all.at[tile, 2], ox_s.at[2], ox_r.at[2], x_dev))
+    start(ends, lambda: (wo, o_all.at[tile, 2], oz_s.at[0], oz_r.at[2], in_dev))
+    start(ends, lambda: (latent, lat_in, ln_s, ln_r, in_dev))
+    start(ends, lambda: (weight, wt_in, wt_s, wt_r, in_dev))
     run(inner, load_o.start)
     start(middle, lambda: (wo, o_all.at[tile, 0], oc_s.at[0, 0], oc_r.at[0, 0], p_dev))
 
@@ -455,15 +469,22 @@
             w_rows(over, 1 - group, at), w_rows(over, 1 - group, at), qc_s.at[1, at], qc_r.at[1 - group, at], p_dev))
 
     def o_first():
-        start(ends, lambda: (
-            wo.at[pl.ds(pl.multiple_of(group * o_half, 16), o_half)], o_rows(tile, 2, group), oz_s.at[0], oz_r.at[2], in_dev))
         start(middle, lambda: (
             wo.at[pl.ds(pl.multiple_of(group * o_half, 16), o_half)], o_rows(tile, 1, group), oz_s.at[1], oz_r.at[1], in_dev))
 
+    def o_end():
+        arrived(outer_end, lambda: o_all.at[over, 2], ox_r.at[2])
+        start(ends, lambda: (o_all.at[over, 2], o_all.at[over, 2], oz_s.at[3], oz_r.at[0], in_dev))
+        arrived(inner, lambda: o_all.at[tile, 2], oz_r.at[2])
+        start(middle, lambda: (o_rows(tile, 2, group), o_rows(tile, 3, group), oz_s.at[2], oz_r.at[3], in_dev))
+        start(middle, lambda: (o_all.at[tile, 2], o_all.at[tile, 2], oc_s.at[0, 2], oc_r.at[0, 2], p_dev))
+
+    def o_end_over():
+        arrived(inner, lambda: o_all.at[over, 2], oz_r.at[0])
+        start(middle, lambda: (o_all.at[over, 2], o_all.at[over, 2], oc_s.at[1, 2], oc_r.at[1, 2], p_dev))
+
     def o_chain(kind):
         arrived(inner, lambda: o_rows(tile, kind, group), oz_r.at[kind])
-        if kind == 2:
-            start(middle, lambda: (o_rows(tile, 2, group), o_rows(tile, 3, group), oz_s.at[2], oz_r.at[3], in_dev))
         start(middle, lambda: (o_rows(tile, kind, group), o_rows(tile, kind, group), ox_s.at[kind], ox_r.at[kind], x_dev))
         start(middle, lambda: (o_rows(tile, kind, group), o_rows(tile, kind, group), oy_s.at[0, kind], oy_r.at[0, kind], y_dev))
 
@@ -499,7 +520,7 @@
 
     strip = 32
 
-    def project(row):
+    def norm_of(row):
         def norm(at, carry):
             rows = pl.ds(pl.multiple_of(at * strip, strip), strip)
             given = n_all[row, rows, :].astype(jnp.float32)
@@ -507,100 +528,91 @@
             return carry
 
         lax.fori_loop(0, block // strip, norm, 0)
+
+    def project(row, pair):
         place_of = pl.ds(pl.multiple_of(row * block, block), block)
-
-        def one(pair, carry):
-            part = jnp.dot(
-                normed[...], w_all[:, pl.ds(pl.multiple_of(pair * (6 * HD), 128), 6 * HD)], preferred_element_type=jnp.float32
-            )
-            for at in (0, 1):
-                here = 3 * HD * at
-                queries[2 * pair + at, place_of, :] = root_norm(part[:, here : here + HD]).astype(queries.dtype)
-                keys[2 * pair + at, place_of, :] = root_norm(part[:, here + HD : here + 2 * HD]).astype(keys.dtype)
-                values[2 * pair + at, place_of, pl.ds(0, HD)] = part[:, here + 2 * HD : here + 3 * HD].astype(values.dtype)
-            return carry
-
-        lax.fori_loop(0, pairs, one, 0)
+        part = jnp.dot(
+            normed[...], w_all[:, pl.ds(pl.multiple_of(pair * (6 * HD), 128), 6 * HD)], preferred_element_type=jnp.float32
+        )
+        for at in (0, 1):
+            here = 3 * HD * at
+            queries[2 * pair + at, place_of, :] = root_norm(part[:, here : here + HD]).astype(queries.dtype)
+            keys[2 * pair + at, place_of, :] = root_norm(part[:, here + HD : here + 2 * HD]).astype(keys.dtype)
+            values[2 * pair + at, place_of, pl.ds(0, HD)] = part[:, here + 2 * HD : here + 3 * HD].astype(values.dtype)
+
+    final = (seqs - 1) * (1 - side)
 
     def in_order(step, carry):
         @pl.when(step == 1)
         def _():
-            o_chain(2)
-
-        @pl.when(step == 3)
+            o_end()
+
+        @pl.when(step == 2)
         def _():
             tokens(2)
-
-        @pl.when(step == 5)
-        def _():
-            o_over(0)
-            o_peer(0, 2)
-            o_over(2)
-            o_chain(1)
-            tokens(3)
 
         far, way = (step + 1) // 2, (step + 1) % 2
         row = place + far * (2 * way - 1)
 
-        @pl.when(both(row >= 0, row < seqs))
-        def _():
-            project(row)
+        @pl.when(both(both(row >= 0, row < seqs), row != final))
+        def _():
+            norm_of(row)
+            lax.fori_loop(0, pairs, lambda pair, carry: (project(row, pair), carry)[1], 0)
 
         return carry
 
-    lax.fori_loop(0, 2 * seqs - 1, in_order, 0)
-
-    def slot_of(row):
-        return row // 2 + 1, 0 if row in (1, 2) else 1
-
-    def kind_at(target):
-        return 2 * outer_end.astype(jnp.int32) + (side != target // 2).astype(jnp.int32)
-
-    def leave(pair, row):
-        target, slot = slot_of(row)
-        kind = kind_at(target)
-        source = attended.at[pair, pl.ds(row * block, block)]
-        landing = att_in.at[kind, pair, pl.ds(slot * block, block)]
-        away = copy(source, landing, at_s.at[row, pair], at_r.at[kind, slot, pair], {"seq": target})
-        stay = pltpu.make_async_copy(source, landing, at_r.at[kind, slot, pair])
-        return place != target, away, place == target, stay
-
-    def one_head(head, carry):
-        pair = head // 2
-        lanes = pl.ds(pl.multiple_of((head % 2) * HD, HD), HD)
-        for row in range(seqs):
-            at = pl.ds(row * block, block)
-            scores = lax.dot_general(
-                queries[head, at, :], keys[head], (((1,), (1,)), ((), ())), preferred_element_type=jnp.float32
-            )
-            expo = jnp.exp2(scores * scale).astype(jnp.bfloat16)
-            mixed = jnp.dot(expo, values[head], preferred_element_type=jnp.float32)
-            attended[pair, at, lanes] = (mixed[:, :HD] * (1.0 / mixed[:, HD:])).astype(attended.dtype)
-
-        @pl.when(head % 2 == 1)
-        def _():
+    lax.fori_loop(0, 2 * seqs - 3, in_order, 0)
+    o_over(0)
+    tokens(3)
+    norm_of(final)
+
+    def leave(pair, turn):
+        row = (turn + 2 * (1 - side)) % seqs
+        target, slot = row // 2 + 1, 1 - ((row + 1) // 2) % 2
+        kind = 2 * outer_end.astype(jnp.int32) + (side != row // 2).astype(jnp.int32)
+        source = attended.at[pair, pl.ds(pl.multiple_of(row * block, block), block)]
+        landing = att_in.at[kind, pair, pl.ds(pl.multiple_of(slot * block, block), block)]
+        got = at_r.at[kind, slot, pair]
+
+        def away():
+            return copy(source, landing, at_s.at[turn, pair], got, {"seq": target})
+
+        def stay():
+            return pltpu.make_async_copy(source, landing, got)
+
+        return place != target, away, stay
+
+    def one_pair(pair, carry):
+        project(final, pair)
+        for half in (0, 1):
+            head = 2 * pair + half
             for row in range(seqs):
-                far, away, near, stay = leave(pair, row)
-                run(far, away.start)
-                run(near, stay.start)
-
-        @pl.when(head == 1)
-        def _():
-            o_peer(1, 2)
-
-        @pl.when(head == heads // 2)
+                at = pl.ds(row * block, block)
+                scores = lax.dot_general(
+                    queries[head, at, :], keys[head], (((1,), (1,)), ((), ())), preferred_element_type=jnp.float32
+                )
+                expo = jnp.exp2(scores * scale).astype(jnp.bfloat16)
+                mixed = jnp.dot(expo, values[head], preferred_element_type=jnp.float32)
+                attended[pair, at, pl.ds(half * HD, HD)] = (mixed[:, :HD] * (1.0 / mixed[:, HD:])).astype(attended.dtype)
+
+        for turn in range(seqs):
+            far, away, stay = leave(pair, turn)
+            run(far, lambda away=away: away().start())
+            run(jnp.logical_not(far), lambda stay=stay: stay().start())
+
+        @pl.when(pair == 0)
+        def _():
+            o_chain(1)
+            o_end_over()
+
+        @pl.when(pair == pairs - 1)
         def _():
             o_chain(3)
             o_over(1)
 
-        @pl.when(head == heads - 1)
-        def _():
-            o_peer(0, 1)
-            o_over(3)
-
         return carry
 
-    lax.fori_loop(0, heads, one_head, 0)
+    lax.fori_loop(0, pairs, one_pair, 0)
 
     @pl.when(inner)
     def _():
@@ -608,59 +620,91 @@
 
     run(inner, load_o.wait)
 
+    def rows_here(kind):
+        copy(o_all.at[mate, kind], o_all.at[mate, kind], oc_s.at[0, kind], oc_r.at[0, kind], p_dev).wait_recv()
+        copy(o_all.at[mate_over, kind], o_all.at[mate_over, kind], oc_s.at[1, kind], oc_r.at[1, kind], p_dev).wait_recv()
+
+    def attended_here(kind, slot, pair):
+        landing = att_in.at[kind, pair, pl.ds(slot * block, block)]
+        copy(landing, landing, at_r.at[kind, slot, pair], at_r.at[kind, slot, pair], p_dev).wait_recv()
+
+    def add_up(kind, which):
+        def columns(owner, carry):
+            here = pl.ds(pl.multiple_of(owner * wo.shape[1], 128), wo.shape[1])
+            total = summed[:, here]
+            for pair in which:
+                rows = pl.ds(pl.multiple_of(pair * 2 * HD, 2 * HD), 2 * HD)
+                total += jnp.dot(att_in[kind, pair], o_all[owner, kind, rows, :], preferred_element_type=jnp.float32)
+            summed[:, here] = total
+            return carry
+
+        lax.fori_loop(0, o_all.shape[0], columns, 0)
+
     def accumulate(kind, carry):
         @pl.when(kind == 1)
         def _():
+            o_peer(0, 1)
+            o_over(3)
             o_peer(1, 1)
 
-        @pl.when(kind == 3)
-        def _():
-            o_peer(0, 3)
-            o_peer(1, 3)
-
         @pl.when(inner)
         def _():
-            copy(o_all.at[mate, kind], o_all.at[mate, kind], oc_s.at[0, kind], oc_r.at[0, kind], p_dev).wait_recv()
-            copy(o_all.at[mate_over, kind], o_all.at[mate_over, kind], oc_s.at[1, kind], oc_r.at[1, kind], p_dev).wait_recv()
-
+            rows_here(kind)
             for slot in (0, 1):
                 for pair in range(pairs):
                     landing = att_in.at[kind, pair, pl.ds(slot * block, block)]
-                    source = attended.at[pair, pl.ds(0, block)]
-                    got = at_r.at[kind, slot, pair]
 
                     @pl.when(kind == 0)
                     def _():
-                        pltpu.make_async_copy(source, landing, got).wait()
+                        pltpu.make_async_copy(attended.at[pair, pl.ds(0, block)], landing, at_r.at[kind, slot, pair]).wait()
 
                     @pl.when(kind != 0)
                     def _():
-                        copy(landing, landing, got, got, p_dev).wait_recv()
-
-            def columns(owner, carry):
-                here = pl.ds(pl.multiple_of(owner * wo.shape[1], 128), wo.shape[1])
-                total = summed[:, here]
-                for pair in range(pairs):
-                    total += jnp.dot(
-                        att_in[kind, pair], o_all[owner, kind, pl.ds(pair * 2 * HD, 2 * HD), :],
-                        preferred_element_type=jnp.float32,
-                    )
-                summed[:, here] = total
-                return carry
-
-            lax.fori_loop(0, o_all.shape[0], columns, 0)
+                        attended_here(kind, slot, pair)
+
+            add_up(kind, range(pairs))
 
         return carry
 
-    lax.fori_loop(0, seqs, accumulate, 0)
-
-    def send_vel():
-        return copy(vel.at[1], vel_in, vl_s, vl_r, out_dev)
+    lax.fori_loop(0, 2, accumulate, 0)
+    o_peer(0, 3)
+    o_peer(1, 3)
+
+    def accumulate_end(at, carry):
+        pair, kind = at // 2, 2 + at % 2
+
+        @pl.when(inner)
+        def _():
+            @pl.when(pair == 0)
+            def _():
+                rows_here(kind)
+
+            for slot in (0, 1):
+                attended_here(kind, slot, pair)
+            add_up(kind, [pair])
+
+        return carry
+
+    lax.fori_loop(0, 2 * pairs, accumulate_end, 0)
+
+    def message(slot):
+        return copy(msg.at[slot], msg_in.at[1 - slot], ms_s.at[slot], ms_r.at[1 - slot], j_dev)
+
+    def answer():
+        return copy(result, result, rs_s, rs_r, out_dev)
+
+    channels = latent.shape[0]
+
+    def level(offset):
+        at = jnp.full((1, block), index[0], jnp.int32).astype(jnp.float32) + offset
+        return noise_level(at, NSTEPS)
 
     @pl.when(inner)
     def _():
-        def finish(step, carry):
-            slot = 1 - step
+        copy(latent, lat_in, ln_s, ln_r, p_dev).wait_recv()
+        copy(weight, wt_in, wt_s, wt_r, p_dev).wait_recv()
+        now, after = level(0.0), level(1.0)
+        for slot in (1, 0):
             row = place - toward * slot
 
             def norm(at, carry):
@@ -671,29 +715,46 @@
                 return carry
 
             lax.fori_loop(0, block // strip, norm, 0)
-            vel[slot] = lax.dot_general(
+            velocity = lax.dot_general(
                 w_head[...], normed[...], (((1,), (1,)), ((), ())), preferred_element_type=jnp.float32
             )
-
-            @pl.when(slot == 1)
-            def _():
-                send_vel().start()
-
-            return carry
-
-        lax.fori_loop(0, 2, finish, 0)
-        velocity[...] = vel[0]
-        send_vel().wait_send()
+            base = (latent if slot == 0 else lat_in)[...]
+            weighs = (weight if slot == 0 else wt_in)[...].astype(jnp.float32)
+            joint[slot, pl.ds(0, channels), :] = (base + (after - now) * velocity) * weighs
+            joint[slot, pl.ds(channels, channels), :] = (base - now * velocity) * weighs
+            msg[slot, pl.ds(0, 2 * channels), :] = joint[slot].astype(msg.dtype)
+            msg[slot, pl.ds(2 * channels, 16), :] = jnp.broadcast_to(weighs, (16, block)).astype(msg.dtype)
+            run(paired, lambda slot=slot: message(slot).start())
+
+        @pl.when(jnp.logical_not(paired))
+        def _():
+            msg_in[...] = jnp.zeros_like(msg_in)
+
+        for slot in (1, 0):
+            run(paired, lambda slot=slot: message(1 - slot).wait_recv())
+            weighs = (weight if slot == 0 else wt_in)[...].astype(jnp.float32)
+            given = msg_in[slot].astype(jnp.float32)
+            joined = (joint[slot] + given[: 2 * channels]) / (weighs + given[2 * channels : 2 * channels + 1])
+            if slot == 1:
+                joint[1] = joined
+                copy(joint.at[1], result, rs_s, rs_r, out_dev).start()
+            else:
+                stepped[...] = joined[:channels]
+                clean[...] = joined[channels:]
+        for slot in (1, 0):
+            run(paired, lambda slot=slot: message(slot).wait_send())
+        copy(joint.at[1], result, rs_s, rs_r, out_dev).wait_send()
 
     @pl.when(outer_end)
     def _():
-        copy(vel_in, vel_in, vl_s, vl_r, p_dev).wait_recv()
-        velocity[...] = vel_in[...]
+        answer().wait_recv()
+        stepped[...] = result[pl.ds(0, channels), :]
+        clean[...] = result[pl.ds(channels, channels), :]
 
     def drain(pair, carry):
-        for row in range(seqs):
-            far, away, _, _ = leave(pair, row)
-            run(far, away.wait_send)
+        for turn in range(seqs):
+            far, away, _ = leave(pair, turn)
+            run(far, lambda away=away: away().wait_send())
         return carry
 
     lax.fori_loop(0, pairs, drain, 0)
@@ -701,19 +762,20 @@
         run(cond(), lambda make=make: copy(*make()).wait_send())
 
 
-def fused(hidden, wq, wo, modulation, w_head):
+def fused(hidden, wq, wo, modulation, w_head, latent, weight, index):
     tiles, seqs = lax.axis_size("tile"), lax.axis_size("seq")
     block, width = hidden.shape
     length, heads = seqs * block, wq.shape[1] // (3 * HD)
     pairs, chunks = heads // 2, 3
-    sizes = [(2, seqs)] * 2 + [(chunks,)] * 4 + [(2, chunks)] * 2 + [()] * 2 + [(3,), (4,)] + [(4,)] * 2 + [(2, 4)] * 4
-    sizes += [(seqs, pairs), (4, 2, pairs), (), ()]
+    channels = w_head.shape[0]
+    sizes = [(2, seqs)] * 2 + [(chunks,)] * 4 + [(2, chunks)] * 2 + [()] * 2 + [(4,)] * 4 + [(2, 4)] * 4
+    sizes += [(seqs, pairs), (4, 2, pairs)] + [()] * 4 + [(2,)] * 2 + [()] * 2
     any_space, vmem = pl.BlockSpec(memory_space=pl.ANY), pl.BlockSpec(memory_space=pltpu.VMEM)
     return pl.pallas_call(
         functools.partial(step_kernel, math.log2(math.e) / math.sqrt(HD)),
-        out_shape=jax.ShapeDtypeStruct((w_head.shape[0], block), jnp.float32),
-        in_specs=[any_space] * 3 + [vmem] * 2,
-        out_specs=vmem,
+        out_shape=(jax.ShapeDtypeStruct((channels, block), jnp.float32),) * 2,
+        in_specs=[any_space] * 3 + [vmem] * 4 + [pl.BlockSpec(memory_space=pltpu.SMEM)],
+        out_specs=(vmem, vmem),
         scratch_shapes=[
             pltpu.VMEM((seqs, block, width), hidden.dtype),
             pltpu.VMEM((block, width), hidden.dtype),
@@ -725,13 +787,17 @@
             pltpu.VMEM((4, pairs, 2 * block, 2 * HD), hidden.dtype),
             pltpu.VMEM((tiles, 4) + wo.shape, wo.dtype),
             pltpu.VMEM((2 * block, width), jnp.float32),
-            pltpu.VMEM((2, w_head.shape[0], block), jnp.float32),
-            pltpu.VMEM((w_head.shape[0], block), jnp.float32),
+            pltpu.VMEM((channels, block), jnp.float32),
+            pltpu.VMEM((1, block), jnp.int32),
+            pltpu.VMEM((2, 2 * channels, block), jnp.float32),
+            pltpu.VMEM((2, 2 * channels + 16, block), jnp.bfloat16),
+            pltpu.VMEM((2, 2 * channels + 16, block), jnp.bfloat16),
+            pltpu.VMEM((2 * channels, block), jnp.float32),
             pltpu.SemaphoreType.DMA((3,)),
         ]
         + [pltpu.SemaphoreType.DMA(shape) for shape in sizes],
         compiler_params=pltpu.CompilerParams(collective_id=1, has_side_effects=True, vmem_limit_bytes=67043328),
-    )(hidden, wq, wo, modulation, w_head)
+    )(hidden, wq, wo, modulation, w_head, latent, weight, index)
 
 
 def fits(hidden, w_qkv, w_out):
@@ -751,9 +817,9 @@
 
 def shards(hidden, modulation, w_qkv, w_out, w_head, latent, weights_int, step_index):
     if fits(hidden, w_qkv, w_out):
-        velocity = fused(hidden[0], w_qkv, w_out, modulation, w_head.T)
-    else:
-        velocity = spread(hidden, modulation, w_qkv, w_out, w_head).T
+        outs = fused(hidden[0], w_qkv, w_out, modulation, w_head.T, latent[0].T, weights_int, step_index)
+        return tuple(out.T[None] for out in outs)
+    velocity = spread(hidden, modulation, w_qkv, w_out, w_head).T
     index = step_index[0].astype(jnp.float32)
     now = noise_level(index, NSTEPS)
     after = noise_level(index + 1.0, NSTEPS)

time: 198 us -> 175 us (0.88)
  starting transfers between devices: 12.8 us -> 0 us
  other arithmetic: 4.23 us -> 0 us
  waiting for transfers between devices: 3.11 us -> 0 us
  Pallas kernels: 174 us -> 171 us
    ppermute x2 -> x0, starting transfers between devices: 12.8 us -> none  [the longest x1 8.93 us: shards(): lax.ppermute(weighted.astype(jnp.bfloat16), ('tile', 'seq'), moves)]
    ppermute x2 -> x0, waiting for transfers between devices: 3.11 us -> none  [the longest x1 3.11 us: shards(): lax.ppermute(weighted.astype(jnp.bfloat16), ('tile', 'seq'), moves)]
    pallas_call x1, Pallas kernels: 174 us -> 171 us  [fused(): pl.pallas_call(functools.partial(step_kernel, math.log2(math.e) / math.sq...]
    unnamed x2, local copies, waits for them, and re-layouts: 0.56 us -> 2.95 us
  transfers between devices with their start and end apart: 2 -> 0, of which waited for: 1 -> 0; matrix products, arithmetic and copies ran while one was open for 1% -> 0% of each run, Pallas kernels for 88% -> 0%
where the time goes in v2:
time: 175 us
  Pallas kernels  171 us (98%)
  local copies, waits for them, and re-layouts  2.95 us (2%)
    pallas_call x1, Pallas kernels, fused(): pl.pallas_call(functools.partial(step_kernel, math.log2(math.e) / math.sq...  171 us

profile of v2, /device:TPU:2, one launch (start us, length us, event | category | flops | bytes accessed | tf_op | source)
XLA Modules:
  0.0 174.9 jit_solution(8698105730889531805)
XLA Ops:
  1.3 170.7 %shard_map.95 = (f32[64,256]{1,0:T(8,128)}, f32[64,256]{1,0:T(8,128)}) custom-call(bf16[256,3072]{1,0:T(8,128)(2,1)} %bitcast.11, bf16[768,2304]{1,0:T(8,128)(2,1)} %wq.1, bf16[768,768]{1,0:T(8,128)(2,1)} %wo.1, f32[5,3072]{1,0:T(8,128)} %modulation.1, bf16[64,3072]{1,0:T(8,128)(2,1)} %bitcast.12, f32[64,256]{1,0:T(8,128)} %bitcast.13, s32[1,256]{1,0:T(1,128)} %weight.1, ...), custom_call_target="tpu_custom_call" | custom-call | tf_op jit(solution)/shard_map/pallas_call | solution.py:774
  172.0 1.5 copy.13
  173.4 1.5 copy.14

commit v3 on v2

--- a/solution.py
+++ b/solution.py
@@ -350,9 +350,9 @@
 
 
 def step_kernel(
-    scale, hidden, wq, wo, modulation, w_head, latent, weight, index, stepped, clean,
+    scale, hidden, wq, wo, mod_from, head_from, latent, weight, index, joined_out,
     n_all, normed, w_all, queries, keys, values, attended, att_in, o_all, summed,
-    lat_in, wt_in, joint, msg, msg_in, result, local,
+    modulation, w_head, lat_in, wt_in, joint, msg, msg_in, result, local,
     nz_s, nz_r, qx_s, qx_r, qy_s, qy_r, qc_s, qc_r, qo_s, qo_r, oz_s, oz_r, ox_s, ox_r, oy_s, oy_r, oc_s, oc_r,
     at_s, at_r, ln_s, ln_r, wt_s, wt_r, ms_s, ms_r, rs_s, rs_r,
 ):
@@ -426,8 +426,9 @@
     def o_rows(owner, kind, part):
         return o_all.at[owner, kind, pl.ds(pl.multiple_of(part * o_half, 16), o_half)]
 
-    loads = [pltpu.make_async_copy(a, b, local.at[k]) for k, (a, b) in enumerate(((hidden, n_all.at[place]), (wq, w_block(tile))))]
-    load_o = pltpu.make_async_copy(wo, o_all.at[tile, 0], local.at[2])
+    given = ((hidden, n_all.at[place]), (wq, w_block(tile)), (mod_from, modulation), (head_from, w_head))
+    loads = [pltpu.make_async_copy(a, b, local.at[k]) for k, (a, b) in enumerate(given)]
+    load_o = pltpu.make_async_copy(wo, o_all.at[tile, 0], local.at[len(loads)])
     for way in (0, 1):
         start(lambda way=way: goes_on(place, seqs, way), lambda way=way: (hidden, n_all.at[place], nz_s.at[way, 1], nz_r.at[way, 1], along(way)))
     for at in range(chunks):
@@ -494,14 +495,22 @@
             start(middle, lambda: (o_all.at[over, 0], o_all.at[over, 0], oc_s.at[1, 0], oc_r.at[1, 0], p_dev))
         else:
             arrived(inner, lambda: o_rows(over, kind, group), ox_r.at[kind])
+        if kind == 3:
             start(middle, lambda: (
                 o_rows(over, kind, group), o_rows(over, kind, group), oy_s.at[1, kind], oy_r.at[1, kind], y_dev))
 
-    def o_peer(which, kind):
-        owner = tile if which == 0 else over
-        arrived(inner, lambda: o_rows(owner, kind, 1 - group), oy_r.at[which, kind])
+    def o_peer(kind):
+        arrived(inner, lambda: o_rows(tile, kind, 1 - group), oy_r.at[0, kind])
+        if kind == 1:
+            start(middle, lambda: (
+                o_rows(tile, kind, 1 - group), o_rows(tile, kind, 1 - group), oy_s.at[1, kind], oy_r.at[1, kind], x_dev))
         start(middle, lambda: (
-            o_all.at[owner, kind], o_all.at[owner, kind], oc_s.at[which, kind], oc_r.at[which, kind], p_dev))
+            o_all.at[tile, kind], o_all.at[tile, kind], oc_s.at[0, kind], oc_r.at[0, kind], p_dev))
+
+    def o_last(kind):
+        arrived(inner, lambda: o_rows(over, kind, 1 - group), oy_r.at[1, kind])
+        start(middle, lambda: (
+            o_all.at[over, kind], o_all.at[over, kind], oc_s.at[1, kind], oc_r.at[1, kind], p_dev))
 
     q_over(0)
     for at in range(1, chunks):
@@ -580,43 +589,36 @@
         def stay():
             return pltpu.make_async_copy(source, landing, got)
 
-        return place != target, away, stay
+        return row, place != target, away, stay
 
     def one_pair(pair, carry):
         project(final, pair)
-        for half in (0, 1):
-            head = 2 * pair + half
-            for row in range(seqs):
-                at = pl.ds(row * block, block)
+        for turn in range(seqs):
+            row, far, away, stay = leave(pair, turn)
+            at = pl.ds(pl.multiple_of(row * block, block), block)
+            for half in (0, 1):
+                head = 2 * pair + half
                 scores = lax.dot_general(
                     queries[head, at, :], keys[head], (((1,), (1,)), ((), ())), preferred_element_type=jnp.float32
                 )
                 expo = jnp.exp2(scores * scale).astype(jnp.bfloat16)
                 mixed = jnp.dot(expo, values[head], preferred_element_type=jnp.float32)
                 attended[pair, at, pl.ds(half * HD, HD)] = (mixed[:, :HD] * (1.0 / mixed[:, HD:])).astype(attended.dtype)
-
-        for turn in range(seqs):
-            far, away, stay = leave(pair, turn)
             run(far, lambda away=away: away().start())
             run(jnp.logical_not(far), lambda stay=stay: stay().start())
 
         @pl.when(pair == 0)
         def _():
             o_chain(1)
-            o_end_over()
 
         @pl.when(pair == pairs - 1)
         def _():
+            o_end_over()
             o_chain(3)
-            o_over(1)
 
         return carry
 
     lax.fori_loop(0, pairs, one_pair, 0)
-
-    @pl.when(inner)
-    def _():
-        summed[...] = jnp.zeros_like(summed)
 
     run(inner, load_o.wait)
 
@@ -628,10 +630,10 @@
         landing = att_in.at[kind, pair, pl.ds(slot * block, block)]
         copy(landing, landing, at_r.at[kind, slot, pair], at_r.at[kind, slot, pair], p_dev).wait_recv()
 
-    def add_up(kind, which):
+    def add_up(kind, which, fresh=False):
         def columns(owner, carry):
             here = pl.ds(pl.multiple_of(owner * wo.shape[1], 128), wo.shape[1])
-            total = summed[:, here]
+            total = 0.0 if fresh else summed[:, here]
             for pair in which:
                 rows = pl.ds(pl.multiple_of(pair * 2 * HD, 2 * HD), 2 * HD)
                 total += jnp.dot(att_in[kind, pair], o_all[owner, kind, rows, :], preferred_element_type=jnp.float32)
@@ -640,38 +642,35 @@
 
         lax.fori_loop(0, o_all.shape[0], columns, 0)
 
-    def accumulate(kind, carry):
-        @pl.when(kind == 1)
+    @pl.when(inner)
+    def _():
+        rows_here(0)
+        for slot in (0, 1):
+            for pair in range(pairs):
+                landing = att_in.at[0, pair, pl.ds(slot * block, block)]
+                pltpu.make_async_copy(attended.at[pair, pl.ds(0, block)], landing, at_r.at[0, slot, pair]).wait()
+        add_up(0, range(pairs), True)
+
+    o_over(1)
+    o_peer(1)
+    o_over(3)
+    o_peer(3)
+
+    def accumulate(at, carry):
+        pair, kind = at // 2, 2 + at % 2
+
+        @pl.when(at == 1)
         def _():
-            o_peer(0, 1)
-            o_over(3)
-            o_peer(1, 1)
-
-        @pl.when(inner)
-        def _():
-            rows_here(kind)
-            for slot in (0, 1):
+            o_last(1)
+            o_last(3)
+
+            @pl.when(inner)
+            def _():
+                rows_here(1)
                 for pair in range(pairs):
-                    landing = att_in.at[kind, pair, pl.ds(slot * block, block)]
-
-                    @pl.when(kind == 0)
-                    def _():
-                        pltpu.make_async_copy(attended.at[pair, pl.ds(0, block)], landing, at_r.at[kind, slot, pair]).wait()
-
-                    @pl.when(kind != 0)
-                    def _():
-                        attended_here(kind, slot, pair)
-
-            add_up(kind, range(pairs))
-
-        return carry
-
-    lax.fori_loop(0, 2, accumulate, 0)
-    o_peer(0, 3)
-    o_peer(1, 3)
-
-    def accumulate_end(at, carry):
-        pair, kind = at // 2, 2 + at % 2
+                    for slot in (0, 1):
+                        attended_here(1, slot, pair)
+                add_up(1, range(pairs))
 
         @pl.when(inner)
         def _():
@@ -685,7 +684,7 @@
 
         return carry
 
-    lax.fori_loop(0, 2 * pairs, accumulate_end, 0)
+    lax.fori_loop(0, 2 * pairs, accumulate, 0)
 
     def message(slot):
         return copy(msg.at[slot], msg_in.at[1 - slot], ms_s.at[slot], ms_r.at[1 - slot], j_dev)
@@ -696,7 +695,7 @@
     channels = latent.shape[0]
 
     def level(offset):
-        at = jnp.full((1, block), index[0], jnp.int32).astype(jnp.float32) + offset
+        at = jnp.broadcast_to(index[...].astype(jnp.float32), (1, block)) + offset
         return noise_level(at, NSTEPS)
 
     @pl.when(inner)
@@ -704,7 +703,7 @@
         copy(latent, lat_in, ln_s, ln_r, p_dev).wait_recv()
         copy(weight, wt_in, wt_s, wt_r, p_dev).wait_recv()
         now, after = level(0.0), level(1.0)
-        for slot in (1, 0):
+        for slot in (0, 1):
             row = place - toward * slot
 
             def norm(at, carry):
@@ -739,8 +738,7 @@
                 joint[1] = joined
                 copy(joint.at[1], result, rs_s, rs_r, out_dev).start()
             else:
-                stepped[...] = joined[:channels]
-                clean[...] = joined[channels:]
+                joined_out[...] = joined
         for slot in (1, 0):
             run(paired, lambda slot=slot: message(slot).wait_send())
         copy(joint.at[1], result, rs_s, rs_r, out_dev).wait_send()
@@ -748,12 +746,11 @@
     @pl.when(outer_end)
     def _():
         answer().wait_recv()
-        stepped[...] = result[pl.ds(0, channels), :]
-        clean[...] = result[pl.ds(channels, channels), :]
+        joined_out[...] = result[...]
 
     def drain(pair, carry):
         for turn in range(seqs):
-            far, away, _ = leave(pair, turn)
+            _, far, away, _ = leave(pair, turn)
             run(far, lambda away=away: away().wait_send())
         return carry
 
@@ -773,9 +770,9 @@
     any_space, vmem = pl.BlockSpec(memory_space=pl.ANY), pl.BlockSpec(memory_space=pltpu.VMEM)
     return pl.pallas_call(
         functools.partial(step_kernel, math.log2(math.e) / math.sqrt(HD)),
-        out_shape=(jax.ShapeDtypeStruct((channels, block), jnp.float32),) * 2,
-        in_specs=[any_space] * 3 + [vmem] * 4 + [pl.BlockSpec(memory_space=pltpu.SMEM)],
-        out_specs=(vmem, vmem),
+        out_shape=jax.ShapeDtypeStruct((2 * channels, block), jnp.float32),
+        in_specs=[any_space] * 5 + [vmem] * 3,
+        out_specs=vmem,
         scratch_shapes=[
             pltpu.VMEM((seqs, block, width), hidden.dtype),
             pltpu.VMEM((block, width), hidden.dtype),
@@ -787,13 +784,15 @@
             pltpu.VMEM((4, pairs, 2 * block, 2 * HD), hidden.dtype),
             pltpu.VMEM((tiles, 4) + wo.shape, wo.dtype),
             pltpu.VMEM((2 * block, width), jnp.float32),
+            pltpu.VMEM(modulation.shape, modulation.dtype),
+            pltpu.VMEM(w_head.shape, w_head.dtype),
             pltpu.VMEM((channels, block), jnp.float32),
             pltpu.VMEM((1, block), jnp.int32),
             pltpu.VMEM((2, 2 * channels, block), jnp.float32),
             pltpu.VMEM((2, 2 * channels + 16, block), jnp.bfloat16),
             pltpu.VMEM((2, 2 * channels + 16, block), jnp.bfloat16),
             pltpu.VMEM((2 * channels, block), jnp.float32),
-            pltpu.SemaphoreType.DMA((3,)),
+            pltpu.SemaphoreType.DMA((5,)),
         ]
         + [pltpu.SemaphoreType.DMA(shape) for shape in sizes],
         compiler_params=pltpu.CompilerParams(collective_id=1, has_side_effects=True, vmem_limit_bytes=67043328),
@@ -817,8 +816,9 @@
 
 def shards(hidden, modulation, w_qkv, w_out, w_head, latent, weights_int, step_index):
     if fits(hidden, w_qkv, w_out):
-        outs = fused(hidden[0], w_qkv, w_out, modulation, w_head.T, latent[0].T, weights_int, step_index)
-        return tuple(out.T[None] for out in outs)
+        joined = fused(hidden[0], w_qkv, w_out, modulation, w_head.T, latent[0].T, weights_int, step_index[None])
+        channels = latent.shape[2]
+        return (joined[:channels].T[None], joined[channels:].T[None])
     velocity = spread(hidden, modulation, w_qkv, w_out, w_head).T
     index = step_index[0].astype(jnp.float32)
     now = noise_level(index, NSTEPS)

time: 175 us -> 167 us (0.954); the launches traced: 175 us -> 164 us
  Pallas kernels: 171 us -> 161 us
    pallas_call x1, Pallas kernels: 171 us -> 161 us  [fused(): pl.pallas_call(functools.partial(step_kernel, math.log2(math.e) / math.sq...]
    unnamed x2 -> x0, local copies, waits for them, and re-layouts: 2.95 us -> none
where the time goes in v3:
time: 167 us; the launch traced here: 164 us
  Pallas kernels  161 us (96%)
    pallas_call x1, Pallas kernels, fused(): pl.pallas_call(functools.partial(step_kernel, math.log2(math.e) / math.sq...  161 us

profile of v3, /device:TPU:2, one launch (start us, length us, event | category | flops | bytes accessed | tf_op | source)
XLA Modules:
  0.0 163.7 jit_solution(2579016851191954732)
XLA Ops:
  1.3 160.8 %shard_map.95 = f32[128,256]{1,0:T(8,128)} custom-call(bf16[256,3072]{1,0:T(8,128)(2,1)} %bitcast.15, bf16[768,2304]{1,0:T(8,128)(2,1)} %wq.1, bf16[768,768]{1,0:T(8,128)(2,1)} %wo.1, f32[5,3072]{1,0:T(8,128)} %mod_from.1, bf16[64,3072]{1,0:T(8,128)(2,1)} %bitcast.16, f32[64,256]{1,0:T(8,128)} %bitcast.17, s32[1,256]{1,0:T(1,128)} %weight.1, ...), custom_call_target="tpu_custom_call" | custom-call | tf_op jit(solution)/shard_map/pallas_call | solution.py:771
  162.1 1.5 slice_bitcast_fusion

commit v4 on v3

--- a/solution.py
+++ b/solution.py
@@ -351,9 +351,9 @@
 
 def step_kernel(
     scale, hidden, wq, wo, mod_from, head_from, latent, weight, index, joined_out,
-    n_all, normed, w_all, queries, keys, values, attended, att_in, o_all, summed,
+    n_all, normed, w_all, w_more, queries, keys, values, attended, att_in, o_all, summed,
     modulation, w_head, lat_in, wt_in, joint, msg, msg_in, result, local,
-    nz_s, nz_r, qx_s, qx_r, qy_s, qy_r, qc_s, qc_r, qo_s, qo_r, oz_s, oz_r, ox_s, ox_r, oy_s, oy_r, oc_s, oc_r,
+    nz_s, nz_r, qx_s, qx_r, qy_s, qy_r, qc_s, qc_r, qo_s, qo_r, oz_s, oz_r, ox_s, ox_r, oy_s, oy_r, oc_s, oc_r, ex_s, ex_r,
     at_s, at_r, ln_s, ln_r, wt_s, wt_r, ms_s, ms_r, rs_s, rs_r,
 ):
     group, tile, place = lax.axis_index("group"), lax.axis_index("tile"), lax.axis_index("seq")
@@ -372,7 +372,7 @@
     q_half, o_half = depth // 2, wo.shape[0] // 2
     chunks = qx_s.shape[0]
     piece = q_half // chunks
-    pairs = attended.shape[0]
+    pairs = attended.shape[0] - 1
     heads = queries.shape[0]
     both = jnp.logical_and
 
@@ -423,8 +423,14 @@
     def w_block(owner):
         return w_all.at[pl.ds(pl.multiple_of(owner * depth, 16), depth)]
 
+    def more_block(owner):
+        return w_more.at[pl.ds(pl.multiple_of(owner * depth, 16), depth)]
+
     def o_rows(owner, kind, part):
         return o_all.at[owner, kind, pl.ds(pl.multiple_of(part * o_half, 16), o_half)]
+
+    def wo_half(part):
+        return wo.at[pl.ds(pl.multiple_of(part * o_half, 16), o_half)]
 
     given = ((hidden, n_all.at[place]), (wq, w_block(tile)), (mod_from, modulation), (head_from, w_head))
     loads = [pltpu.make_async_copy(a, b, local.at[k]) for k, (a, b) in enumerate(given)]
@@ -438,9 +444,11 @@
     for load in loads:
         load.start()
     start(yes, lambda: (wq, w_block(tile), qo_s, qo_r, p_dev))
-    start(middle, lambda: (wo, o_all.at[tile, 0], ox_s.at[0], ox_r.at[0], x_dev))
+    start(middle, lambda: (wo_half(group), o_rows(tile, 0, group), ox_s.at[0], ox_r.at[0], x_dev))
     start(ends, lambda: (wo, o_all.at[tile, 2], ox_s.at[2], ox_r.at[2], x_dev))
-    start(ends, lambda: (wo, o_all.at[tile, 2], oz_s.at[0], oz_r.at[2], in_dev))
+    start(ends, lambda: (wq.at[:, pl.ds((pairs - 1) * 6 * HD, 6 * HD)], more_block(tile), ex_s.at[0], ex_r.at[0], in_dev))
+    start(ends, lambda: (wo_half(group), o_rows(tile, 2, group), oz_s.at[0], oz_r.at[2], in_dev))
+    start(ends, lambda: (wo_half(1 - group), o_rows(tile, 2, 1 - group), ex_s.at[4], ex_r.at[4], in_dev))
     start(ends, lambda: (latent, lat_in, ln_s, ln_r, in_dev))
     start(ends, lambda: (weight, wt_in, wt_s, wt_r, in_dev))
     run(inner, load_o.start)
@@ -470,14 +478,27 @@
             w_rows(over, 1 - group, at), w_rows(over, 1 - group, at), qc_s.at[1, at], qc_r.at[1 - group, at], p_dev))
 
     def o_first():
-        start(middle, lambda: (
-            wo.at[pl.ds(pl.multiple_of(group * o_half, 16), o_half)], o_rows(tile, 1, group), oz_s.at[1], oz_r.at[1], in_dev))
+        start(middle, lambda: (wo_half(group), o_rows(tile, 1, group), oz_s.at[1], oz_r.at[1], in_dev))
+
+    def more():
+        arrived(inner, lambda: more_block(tile), ex_r.at[0])
+        start(middle, lambda: (more_block(tile), more_block(tile), ex_s.at[1], ex_r.at[1], x_dev))
+        start(middle, lambda: (more_block(tile), more_block(tile), ex_s.at[2], ex_r.at[2], p_dev))
+
+    def more_over():
+        arrived(inner, lambda: more_block(over), ex_r.at[1])
+        start(middle, lambda: (more_block(over), more_block(over), ex_s.at[3], ex_r.at[3], p_dev))
 
     def o_end():
         arrived(outer_end, lambda: o_all.at[over, 2], ox_r.at[2])
         start(ends, lambda: (o_all.at[over, 2], o_all.at[over, 2], oz_s.at[3], oz_r.at[0], in_dev))
-        arrived(inner, lambda: o_all.at[tile, 2], oz_r.at[2])
+
+    def o_end_far():
+        arrived(inner, lambda: o_rows(tile, 2, group), oz_r.at[2])
         start(middle, lambda: (o_rows(tile, 2, group), o_rows(tile, 3, group), oz_s.at[2], oz_r.at[3], in_dev))
+
+    def o_end_own():
+        arrived(inner, lambda: o_rows(tile, 2, 1 - group), ex_r.at[4])
         start(middle, lambda: (o_all.at[tile, 2], o_all.at[tile, 2], oc_s.at[0, 2], oc_r.at[0, 2], p_dev))
 
     def o_end_over():
@@ -490,12 +511,8 @@
         start(middle, lambda: (o_rows(tile, kind, group), o_rows(tile, kind, group), oy_s.at[0, kind], oy_r.at[0, kind], y_dev))
 
     def o_over(kind):
-        if kind == 0:
-            arrived(inner, lambda: o_all.at[over, 0], ox_r.at[0])
-            start(middle, lambda: (o_all.at[over, 0], o_all.at[over, 0], oc_s.at[1, 0], oc_r.at[1, 0], p_dev))
-        else:
-            arrived(inner, lambda: o_rows(over, kind, group), ox_r.at[kind])
-        if kind == 3:
+        arrived(inner, lambda: o_rows(over, kind, group), ox_r.at[kind])
+        if kind != 1:
             start(middle, lambda: (
                 o_rows(over, kind, group), o_rows(over, kind, group), oy_s.at[1, kind], oy_r.at[1, kind], y_dev))
 
@@ -538,11 +555,10 @@
 
         lax.fori_loop(0, block // strip, norm, 0)
 
-    def project(row, pair):
+    def project(row, pair, extra=False):
         place_of = pl.ds(pl.multiple_of(row * block, block), block)
-        part = jnp.dot(
-            normed[...], w_all[:, pl.ds(pl.multiple_of(pair * (6 * HD), 128), 6 * HD)], preferred_element_type=jnp.float32
-        )
+        weights = w_more[...] if extra else w_all[:, pl.ds(pl.multiple_of(pair * (6 * HD), 128), 6 * HD)]
+        part = jnp.dot(normed[...], weights, preferred_element_type=jnp.float32)
         for at in (0, 1):
             here = 3 * HD * at
             queries[2 * pair + at, place_of, :] = root_norm(part[:, here : here + HD]).astype(queries.dtype)
@@ -554,6 +570,8 @@
     def in_order(step, carry):
         @pl.when(step == 1)
         def _():
+            o_over(0)
+            more()
             o_end()
 
         @pl.when(step == 2)
@@ -571,54 +589,92 @@
         return carry
 
     lax.fori_loop(0, 2 * seqs - 3, in_order, 0)
-    o_over(0)
+    o_end_far()
+    o_last(0)
     tokens(3)
     norm_of(final)
 
-    def leave(pair, turn):
+    def leave(step, turn):
+        extra = step // pairs
         row = (turn + 2 * (1 - side)) % seqs
         target, slot = row // 2 + 1, 1 - ((row + 1) // 2) % 2
-        kind = 2 * outer_end.astype(jnp.int32) + (side != row // 2).astype(jnp.int32)
-        source = attended.at[pair, pl.ds(pl.multiple_of(row * block, block), block)]
-        landing = att_in.at[kind, pair, pl.ds(pl.multiple_of(slot * block, block), block)]
-        got = at_r.at[kind, slot, pair]
+        kind = (side != row // 2).astype(jnp.int32) + 2 * (extra + outer_end.astype(jnp.int32))
+        source = attended.at[step, pl.ds(pl.multiple_of(row * block, block), block)]
+        landing = att_in.at[kind, step - extra, pl.ds(pl.multiple_of(slot * block, block), block)]
+        got = at_r.at[kind, slot, step - extra]
 
         def away():
-            return copy(source, landing, at_s.at[turn, pair], got, {"seq": target})
+            return copy(source, landing, at_s.at[turn, step], got, {"seq": target})
 
         def stay():
             return pltpu.make_async_copy(source, landing, got)
 
         return row, place != target, away, stay
 
-    def one_pair(pair, carry):
-        project(final, pair)
+    def attend(step):
         for turn in range(seqs):
-            row, far, away, stay = leave(pair, turn)
+            row, far, away, stay = leave(step, turn)
             at = pl.ds(pl.multiple_of(row * block, block), block)
             for half in (0, 1):
-                head = 2 * pair + half
+                head = 2 * (step % pairs) + half
                 scores = lax.dot_general(
                     queries[head, at, :], keys[head], (((1,), (1,)), ((), ())), preferred_element_type=jnp.float32
                 )
                 expo = jnp.exp2(scores * scale).astype(jnp.bfloat16)
                 mixed = jnp.dot(expo, values[head], preferred_element_type=jnp.float32)
-                attended[pair, at, pl.ds(half * HD, HD)] = (mixed[:, :HD] * (1.0 / mixed[:, HD:])).astype(attended.dtype)
+                attended[step, at, pl.ds(half * HD, HD)] = (mixed[:, :HD] * (1.0 / mixed[:, HD:])).astype(attended.dtype)
             run(far, lambda away=away: away().start())
             run(jnp.logical_not(far), lambda stay=stay: stay().start())
 
-        @pl.when(pair == 0)
+    def mine(step):
+        return jnp.logical_or(inner, step < pairs - 1)
+
+    def one_more(step, carry):
+        row = (final + step) % seqs
+
+        @pl.when(step == 1)
+        def _():
+            o_chain(3)
+            o_over(1)
+            o_peer(1)
+
+        @pl.when(step > 0)
+        def _():
+            norm_of(row)
+
+        project(row, 0, True)
+        return carry
+
+    def one_pair(step, carry):
+        @pl.when(both(mine(step), step < pairs))
+        def _():
+            project(final, step)
+
+        @pl.when(both(inner, step == pairs))
+        def _():
+            copy(more_block(mate), more_block(mate), ex_s.at[2], ex_r.at[2], p_dev).wait_recv()
+            copy(more_block(mate_over), more_block(mate_over), ex_s.at[3], ex_r.at[3], p_dev).wait_recv()
+            lax.fori_loop(0, seqs, one_more, 0)
+            o_over(3)
+            o_peer(3)
+
+        @pl.when(mine(step))
+        def _():
+            attend(step)
+
+        @pl.when(step == 0)
         def _():
             o_chain(1)
-
-        @pl.when(pair == pairs - 1)
-        def _():
-            o_end_over()
-            o_chain(3)
+            o_end_own()
+
+        @pl.when(step == 1)
+        def _():
+            more_over()
 
         return carry
 
-    lax.fori_loop(0, pairs, one_pair, 0)
+    lax.fori_loop(0, pairs + 1, one_pair, 0)
+    o_end_over()
 
     run(inner, load_o.wait)
 
@@ -631,16 +687,20 @@
         copy(landing, landing, at_r.at[kind, slot, pair], at_r.at[kind, slot, pair], p_dev).wait_recv()
 
     def add_up(kind, which, fresh=False):
-        def columns(owner, carry):
-            here = pl.ds(pl.multiple_of(owner * wo.shape[1], 128), wo.shape[1])
+        cut = 2 if wo.shape[1] % 256 == 0 else 1
+        wide = wo.shape[1] // cut
+
+        def columns(at, carry):
+            owner, some = at // cut, pl.ds(pl.multiple_of(at % cut * wide, 128), wide)
+            here = pl.ds(pl.multiple_of(at * wide, 128), wide)
             total = 0.0 if fresh else summed[:, here]
             for pair in which:
                 rows = pl.ds(pl.multiple_of(pair * 2 * HD, 2 * HD), 2 * HD)
-                total += jnp.dot(att_in[kind, pair], o_all[owner, kind, rows, :], preferred_element_type=jnp.float32)
+                total += jnp.dot(att_in[kind, pair], o_all[owner, kind, rows, some], preferred_element_type=jnp.float32)
             summed[:, here] = total
             return carry
 
-        lax.fori_loop(0, o_all.shape[0], columns, 0)
+        lax.fori_loop(0, cut * o_all.shape[0], columns, 0)
 
     @pl.when(inner)
     def _():
@@ -651,40 +711,41 @@
                 pltpu.make_async_copy(attended.at[pair, pl.ds(0, block)], landing, at_r.at[0, slot, pair]).wait()
         add_up(0, range(pairs), True)
 
-    o_over(1)
-    o_peer(1)
-    o_over(3)
-    o_peer(3)
-
-    def accumulate(at, carry):
-        pair, kind = at // 2, 2 + at % 2
-
-        @pl.when(at == 1)
-        def _():
-            o_last(1)
-            o_last(3)
-
-            @pl.when(inner)
-            def _():
-                rows_here(1)
-                for pair in range(pairs):
-                    for slot in (0, 1):
-                        attended_here(1, slot, pair)
-                add_up(1, range(pairs))
-
-        @pl.when(inner)
-        def _():
-            @pl.when(pair == 0)
-            def _():
-                rows_here(kind)
-
+    def from_end(pair, kind):
+        for slot in (0, 1):
+            attended_here(kind, slot, pair)
+        add_up(kind, [pair])
+
+    @pl.when(inner)
+    def _():
+        rows_here(2)
+        for slot in (0, 1):
+            landing = att_in.at[2, pairs - 1, pl.ds(slot * block, block)]
+            pltpu.make_async_copy(attended.at[pairs, pl.ds(0, block)], landing, at_r.at[2, slot, pairs - 1]).wait()
+        add_up(2, [pairs - 1])
+        from_end(0, 2)
+
+    o_last(1)
+    o_last(3)
+
+    @pl.when(inner)
+    def _():
+        rows_here(1)
+        for pair in range(pairs):
             for slot in (0, 1):
-                attended_here(kind, slot, pair)
-            add_up(kind, [pair])
-
-        return carry
-
-    lax.fori_loop(0, 2 * pairs, accumulate, 0)
+                attended_here(1, slot, pair)
+        add_up(1, range(pairs))
+        rows_here(3)
+        for slot in (0, 1):
+            attended_here(3, slot, pairs - 1)
+            attended_here(3, slot, 0)
+        add_up(3, [0, pairs - 1])
+
+        def later(at, carry):
+            from_end(1 + at // 2, 2 + at % 2)
+            return carry
+
+        lax.fori_loop(0, 2 * (pairs - 2), later, 0)
 
     def message(slot):
         return copy(msg.at[slot], msg_in.at[1 - slot], ms_s.at[slot], ms_r.at[1 - slot], j_dev)
@@ -748,13 +809,13 @@
         answer().wait_recv()
         joined_out[...] = result[...]
 
-    def drain(pair, carry):
+    def drain(step, carry):
         for turn in range(seqs):
-            _, far, away, _ = leave(pair, turn)
-            run(far, lambda away=away: away().wait_send())
+            _, far, away, _ = leave(step, turn)
+            run(both(far, mine(step)), lambda away=away: away().wait_send())
         return carry
 
-    lax.fori_loop(0, pairs, drain, 0)
+    lax.fori_loop(0, pairs + 1, drain, 0)
     for cond, make in sent:
         run(cond(), lambda make=make: copy(*make()).wait_send())
 
@@ -765,8 +826,8 @@
     length, heads = seqs * block, wq.shape[1] // (3 * HD)
     pairs, chunks = heads // 2, 3
     channels = w_head.shape[0]
-    sizes = [(2, seqs)] * 2 + [(chunks,)] * 4 + [(2, chunks)] * 2 + [()] * 2 + [(4,)] * 4 + [(2, 4)] * 4
-    sizes += [(seqs, pairs), (4, 2, pairs)] + [()] * 4 + [(2,)] * 2 + [()] * 2
+    sizes = [(2, seqs)] * 2 + [(chunks,)] * 4 + [(2, chunks)] * 2 + [()] * 2 + [(4,)] * 4 + [(2, 4)] * 4 + [(5,)] * 2
+    sizes += [(seqs, pairs + 1), (4, 2, pairs)] + [()] * 4 + [(2,)] * 2 + [()] * 2
     any_space, vmem = pl.BlockSpec(memory_space=pl.ANY), pl.BlockSpec(memory_space=pltpu.VMEM)
     return pl.pallas_call(
         functools.partial(step_kernel, math.log2(math.e) / math.sqrt(HD)),
@@ -777,10 +838,11 @@
             pltpu.VMEM((seqs, block, width), hidden.dtype),
             pltpu.VMEM((block, width), hidden.dtype),
             pltpu.VMEM((tiles * wq.shape[0], wq.shape[1]), wq.dtype),
+            pltpu.VMEM((tiles * wq.shape[0], 6 * HD), wq.dtype),
             pltpu.VMEM((heads, length, HD), hidden.dtype),
             pltpu.VMEM((heads, length, HD), hidden.dtype),
             pltpu.VMEM((heads, length, 2 * HD), hidden.dtype),
-            pltpu.VMEM((pairs, length, 2 * HD), hidden.dtype),
+            pltpu.VMEM((pairs + 1, length, 2 * HD), hidden.dtype),
             pltpu.VMEM((4, pairs, 2 * block, 2 * HD), hidden.dtype),
             pltpu.VMEM((tiles, 4) + wo.shape, wo.dtype),
             pltpu.VMEM((2 * block, width), jnp.float32),
@@ -802,7 +864,7 @@
 def fits(hidden, w_qkv, w_out):
     sizes = tuple(lax.axis_size(name) for name in ("group", "tile", "seq"))
     heads = w_qkv.shape[1] // (3 * HD)
-    return sizes == (2, 4, 4) and heads % 2 == 0 and w_out.shape[1] % 128 == 0 and w_qkv.shape[0] % 96 == 0
+    return sizes == (2, 4, 4) and heads % 2 == 0 and heads >= 4 and w_out.shape[1] % 128 == 0 and w_qkv.shape[0] % 96 == 0
 
 
 def spread(hidden, modulation, w_qkv, w_out, w_head):

time: 167 us -> 165 us (0.988); the launches traced: 164 us -> 165 us
  no operation moved by 1% of the time
where the time goes in v4:
time: 165 us
  Pallas kernels  162 us (98%)
    pallas_call x1, Pallas kernels, fused(): pl.pallas_call(functools.partial(step_kernel, math.log2(math.e) / math.sq...  162 us

profile of v4, /device:TPU:2, one launch (start us, length us, event | category | flops | bytes accessed | tf_op | source)
XLA Modules:
  0.0 164.7 jit_solution(14551409411213924805)
XLA Ops:
  1.3 161.9 %shard_map.95 = f32[128,256]{1,0:T(8,128)} custom-call(bf16[256,3072]{1,0:T(8,128)(2,1)} %bitcast.15, bf16[768,2304]{1,0:T(8,128)(2,1)} %wq.1, bf16[768,768]{1,0:T(8,128)(2,1)} %wo.1, f32[5,3072]{1,0:T(8,128)} %mod_from.1, bf16[64,3072]{1,0:T(8,128)(2,1)} %bitcast.16, f32[64,256]{1,0:T(8,128)} %bitcast.17, s32[1,256]{1,0:T(1,128)} %weight.1, ...), custom_call_target="tpu_custom_call" | custom-call | tf_op jit(solution)/shard_map/pallas_call | solution.py:832
  163.2 1.5 slice_bitcast_fusion
